TPU v7x, 32 devices: a whole 2x2x4 slice. The times are simulated.
32 devices in a mesh: dp: 4 (over z), ctx: 2 (over x), head: 4 (over y, core).
Axes of the slice: x: 2, y: 2, z: 4, core: 2. Of those that a mesh axis runs over, the one named last changes fastest.
Arguments:
- block_in: bfloat16 [4096, 640], P(('dp', 'ctx', 'head')), may hold values from -6 to 6
- cotangent: bfloat16 [4096, 640], P(('dp', 'ctx', 'head')), may hold values from -6 to 6
- positions: int32 [4096], P(('dp', 'ctx')), may hold values from 0 to 1023, as said below
- norm_gains: float32 [4, 640], replicated, may hold values from 0.5 to 1.5
- qk_gains: float32 [2, 256], replicated, may hold values from 0.5 to 1.5
- w_query: bfloat16 [640, 1024], P(None, ('dp', 'ctx', 'head')), may hold values from -0.25 to 0.25
- w_key: bfloat16 [640, 256], P(None, ('dp', 'ctx', 'head')), may hold values from -0.25 to 0.25
- w_value: bfloat16 [640, 256], P(None, ('dp', 'ctx', 'head')), may hold values from -0.25 to 0.25
- w_out: bfloat16 [1024, 640], P(('dp', 'ctx', 'head')), may hold values from -0.75 to 0.75
- w_gate: bfloat16 [640, 2048], P(None, ('dp', 'ctx', 'head')), may hold values from -0.25 to 0.25
- w_up: bfloat16 [640, 2048], P(None, ('dp', 'ctx', 'head')), may hold values from -0.25 to 0.25
- w_down: bfloat16 [2048, 640], P(('dp', 'ctx', 'head')), may hold values from -0.125 to 0.125
Outputs:
- block_out: bfloat16 [4096, 640], P(('dp', 'ctx', 'head'))
- d_block_in: bfloat16 [4096, 640], P(('dp', 'ctx', 'head'))
- grad_norm_gains: float32 [4, 640], replicated
- grad_qk_gains: float32 [2, 256], replicated
- grad_query: float32 [640, 1024], P(None, ('dp', 'ctx', 'head'))
- grad_key: float32 [640, 256], P(None, ('dp', 'ctx', 'head'))
- grad_value: float32 [640, 256], P(None, ('dp', 'ctx', 'head'))
- grad_out: float32 [1024, 640], P(('dp', 'ctx', 'head'))
- grad_gate: float32 [640, 2048], P(None, ('dp', 'ctx', 'head'))
- grad_up: float32 [640, 2048], P(None, ('dp', 'ctx', 'head'))
- grad_down: float32 [2048, 640], P(('dp', 'ctx', 'head'))
Inputs may be any that keep to these rules, and one draw needn't show every extreme that they name: Each sequence of 1024 tokens holds one or two documents: positions count from 0 at the sequence's first token and restart from 0 at most once.
All inputs are finite; a program needn't handle non-finite values.
Results may differ from a plain program's by a relative error of at most 0.019.
Values may be sent and summed in bfloat16 or wider, within the bound.
A program may use at most 128 MiB of HBM per device.

v0:
```python
import math

import jax
import jax.numpy as jnp
from jax import lax
from jax.sharding import PartitionSpec as P

epsilon = 1e-06
rope_base = 1000000.0
score_scale = 0.0625
negative_fill = -1e30


def norm_rows(values, gain_vec):
    inverse = lax.rsqrt(jnp.mean(values * values, axis=-1, keepdims=True) + epsilon)
    return (values * inverse * gain_vec, inverse)


def norm_back(values, inverse, gain_vec, upstream):
    scaled = upstream * gain_vec
    inner_mean = jnp.mean(scaled * values, axis=-1, keepdims=True)
    return (
        inverse * scaled - values * (inverse * inverse * inverse) * inner_mean,
        upstream * values * inverse,
    )


def rope_angles(positions, full_width):
    ladder = jnp.arange(full_width // 2, dtype=jnp.float32)
    frequency = jnp.exp(ladder * (-2.0 / full_width) * math.log(rope_base))
    angles = positions.astype(jnp.float32)[:, None] * frequency[None, :]
    return (jnp.cos(angles), jnp.sin(angles))


def rotate(values, cosine, sine_part):
    middle = values.shape[-1] // 2
    first_half = values[..., :middle]
    second = values[..., middle:]
    return jnp.concatenate(
        [first_half * cosine - second * sine_part, second * cosine + first_half * sine_part],
        axis=-1,
    )


def gelu_product(gate_pre, up_pre):
    return jax.nn.gelu(gate_pre, approximate=True) * up_pre


def split_columns(values, group_count, inner_count):
    width = values.shape[1]
    return values.reshape(
        values.shape[0], group_count, inner_count, width // (group_count * inner_count)
    )


def weight_terms(rows_all, cols_all, group_count):
    attn_rows, mlp_rows, branch_rows, down_rows = rows_all
    merged = [piece.reshape(piece.shape[0], group_count, piece.shape[3]) for piece in cols_all]
    query_cols, key_cols, value_cols, gate_cols, up_cols, out_cols, hidden_cols = merged
    query_terms = jnp.einsum(
        "td,tgs->dgs", attn_rows, query_cols, preferred_element_type=jnp.float32
    )
    key_terms = jnp.einsum("td,tgs->dgs", attn_rows, key_cols, preferred_element_type=jnp.float32)
    value_terms = jnp.einsum(
        "td,tgs->dgs", attn_rows, value_cols, preferred_element_type=jnp.float32
    )
    gate_terms = jnp.einsum("td,tgs->dgs", mlp_rows, gate_cols, preferred_element_type=jnp.float32)
    up_terms = jnp.einsum("td,tgs->dgs", mlp_rows, up_cols, preferred_element_type=jnp.float32)
    out_terms = jnp.einsum("tgs,td->gsd", out_cols, branch_rows, preferred_element_type=jnp.float32)
    down_terms = jnp.einsum(
        "tgs,td->gsd", hidden_cols, down_rows, preferred_element_type=jnp.float32
    )
    return (query_terms, key_terms, value_terms, gate_terms, up_terms, out_terms, down_terms)


def owned_slices(summed, model_width):
    column_owned = [piece.reshape(model_width, piece.shape[2]) for piece in summed[:5]]
    row_owned = [piece.reshape(piece.shape[1], model_width) for piece in summed[5:]]
    return column_owned + row_owned


def local(
    block_in,
    cotangent,
    positions,
    norm_gains,
    qk_gains,
    w_query,
    w_key,
    w_value,
    w_out,
    w_gate,
    w_up,
    w_down,
):
    tok_rows = block_in.shape[0]
    model_width = block_in.shape[1]
    head_count = lax.axis_size("head")
    head_width = qk_gains.shape[1]
    head_slot = lax.axis_index("head")
    ctx_slot = lax.axis_index("ctx")
    query_rows = head_count * tok_rows
    own_positions = lax.dynamic_slice_in_dim(positions, head_slot * tok_rows, tok_rows)
    full_query, full_key, full_value, full_out = (
        lax.all_gather(w_query, ("dp", "ctx", "head"), axis=1, tiled=True),
        lax.all_gather(w_key, ("dp", "ctx", "head"), axis=1, tiled=True),
        lax.all_gather(w_value, ("dp", "ctx", "head"), axis=1, tiled=True),
        lax.all_gather(w_out, ("dp", "ctx", "head"), axis=0, tiled=True),
    )
    input_wide = block_in.astype(jnp.float32)
    attn_norm, inverse_in = norm_rows(input_wide, norm_gains[0])
    attn_in = attn_norm.astype(jnp.bfloat16)
    query_raw = jnp.dot(attn_in, full_query, preferred_element_type=jnp.float32).reshape(
        tok_rows, head_count, head_width
    )
    key_raw = jnp.dot(attn_in, full_key, preferred_element_type=jnp.float32)
    value_rows = jnp.dot(attn_in, full_value, preferred_element_type=jnp.float32).astype(
        jnp.bfloat16
    )
    query_normed, inverse_query = norm_rows(query_raw, qk_gains[0])
    key_normed, inverse_key = norm_rows(key_raw, qk_gains[1])
    cosine, sine_part = rope_angles(own_positions, head_width)
    rot_query = (rotate(query_normed, cosine[:, None], sine_part[:, None]) * score_scale).astype(
        jnp.bfloat16
    )
    rot_key = rotate(key_normed, cosine, sine_part).astype(jnp.bfloat16)
    head_query = lax.all_to_all(rot_query, "head", split_axis=1, concat_axis=0, tiled=True).reshape(
        query_rows, head_width
    )
    all_keys, all_values = (
        lax.all_gather(rot_key, ("ctx", "head"), axis=0, tiled=True),
        lax.all_gather(value_rows, ("ctx", "head"), axis=0, tiled=True),
    )
    first_query = ctx_slot * query_rows
    query_index = first_query + jnp.arange(query_rows, dtype=jnp.int32)
    lowest_key = query_index - positions
    key_block = min(512, query_rows)
    block_count = (ctx_slot + 1) * (query_rows // key_block)

    def block_scores(block_index):
        key_start = block_index * key_block
        keys_here = lax.dynamic_slice_in_dim(all_keys, key_start, key_block)
        scores = jnp.einsum("qd,kd->qk", head_query, keys_here, preferred_element_type=jnp.float32)
        key_index = key_start + jnp.arange(key_block, dtype=jnp.int32)
        visible = (key_index[None, :] <= query_index[:, None]) & (
            key_index[None, :] >= lowest_key[:, None]
        )
        return (jnp.where(visible, scores, negative_fill), visible, key_start, keys_here)

    def running_total(block_index, carry):
        top_now, total_now = carry
        scores, visible, _, _ = block_scores(block_index)
        top_new = jnp.maximum(top_now, jnp.max(scores, axis=1))
        weights = jnp.where(visible, jnp.exp(scores - top_new[:, None]), 0.0)
        return (top_new, total_now * jnp.exp(top_now - top_new) + jnp.sum(weights, axis=1))

    start_top = jnp.full((query_rows,), negative_fill, jnp.float32)
    top_all, total_all = lax.fori_loop(
        0, block_count, running_total, (start_top, jnp.zeros((query_rows,), jnp.float32))
    )
    log_total = top_all + jnp.log(total_all)

    def weighted_sum(block_index, accumulated):
        scores, _, key_start, _ = block_scores(block_index)
        prob_rows = jnp.exp(scores - log_total[:, None]).astype(jnp.bfloat16)
        values_here = lax.dynamic_slice_in_dim(all_values, key_start, key_block)
        return accumulated + jnp.dot(prob_rows, values_here, preferred_element_type=jnp.float32)

    attn_exact = lax.fori_loop(
        0, block_count, weighted_sum, jnp.zeros((query_rows, head_width), jnp.float32)
    )
    attn_back = lax.all_to_all(
        attn_exact.astype(jnp.bfloat16).reshape(query_rows, 1, head_width),
        "head",
        split_axis=0,
        concat_axis=1,
        tiled=True,
    )
    attn_out = attn_back.reshape(tok_rows, head_count * head_width)
    branch = jnp.dot(attn_out, full_out, preferred_element_type=jnp.float32)
    branch_normed, inverse_branch = norm_rows(branch, norm_gains[1])
    middle = input_wide + branch_normed
    mlp_norm, inverse_mid = norm_rows(middle, norm_gains[2])
    mlp_in = mlp_norm.astype(jnp.bfloat16)
    full_gate, full_up, full_down = (
        lax.all_gather(w_gate, ("dp", "ctx", "head"), axis=1, tiled=True),
        lax.all_gather(w_up, ("dp", "ctx", "head"), axis=1, tiled=True),
        lax.all_gather(w_down, ("dp", "ctx", "head"), axis=0, tiled=True),
    )
    gate_pre = jnp.dot(mlp_in, full_gate, preferred_element_type=jnp.float32)
    up_pre = jnp.dot(mlp_in, full_up, preferred_element_type=jnp.float32)
    hidden = gelu_product(gate_pre, up_pre).astype(jnp.bfloat16)
    down_raw = jnp.dot(hidden, full_down, preferred_element_type=jnp.float32)
    down_normed, inverse_down = norm_rows(down_raw, norm_gains[3])
    block_out = (middle + down_normed).astype(jnp.bfloat16)
    cot_wide = cotangent.astype(jnp.float32)
    grad_down_raw, gain_three = norm_back(down_raw, inverse_down, norm_gains[3], cot_wide)
    grad_down_in = grad_down_raw.astype(jnp.bfloat16)
    grad_hidden = jnp.einsum(
        "td,fd->tf", grad_down_in, full_down, preferred_element_type=jnp.float32
    )
    _, gelu_pull = jax.vjp(gelu_product, gate_pre, up_pre)
    grad_gate_raw, grad_up_raw = gelu_pull(grad_hidden)
    grad_gate_in = grad_gate_raw.astype(jnp.bfloat16)
    grad_up_in = grad_up_raw.astype(jnp.bfloat16)
    grad_mlp_in = jnp.einsum(
        "tf,df->td", grad_gate_in, full_gate, preferred_element_type=jnp.float32
    )
    grad_mlp_in = grad_mlp_in + jnp.einsum(
        "tf,df->td", grad_up_in, full_up, preferred_element_type=jnp.float32
    )
    grad_mid_part, gain_two = norm_back(middle, inverse_mid, norm_gains[2], grad_mlp_in)
    grad_middle = cot_wide + grad_mid_part
    grad_branch_raw, gain_one = norm_back(branch, inverse_branch, norm_gains[1], grad_middle)
    grad_branch = grad_branch_raw.astype(jnp.bfloat16)
    grad_attn = jnp.einsum(
        "td,ed->te", grad_branch, full_out, preferred_element_type=jnp.float32
    ).astype(jnp.bfloat16)
    head_grad = lax.all_to_all(
        grad_attn.reshape(tok_rows, head_count, head_width),
        "head",
        split_axis=1,
        concat_axis=0,
        tiled=True,
    ).reshape(query_rows, head_width)
    row_delta = jnp.sum(head_grad.astype(jnp.float32) * attn_exact, axis=1)

    def block_grads(block_index, carry):
        query_acc, key_acc, value_acc = carry
        scores, _, key_start, keys_here = block_scores(block_index)
        probs_wide = jnp.exp(scores - log_total[:, None])
        prob_rows = probs_wide.astype(jnp.bfloat16)
        values_here = lax.dynamic_slice_in_dim(all_values, key_start, key_block)
        value_part = jnp.einsum(
            "qk,qd->kd", prob_rows, head_grad, preferred_element_type=jnp.float32
        )
        grad_probs = jnp.einsum(
            "qd,kd->qk", head_grad, values_here, preferred_element_type=jnp.float32
        )
        grad_scores = (probs_wide * (grad_probs - row_delta[:, None])).astype(jnp.bfloat16)
        query_acc = query_acc + jnp.dot(grad_scores, keys_here, preferred_element_type=jnp.float32)
        key_part = jnp.einsum(
            "qk,qd->kd", grad_scores, head_query, preferred_element_type=jnp.float32
        )
        key_acc = lax.dynamic_update_slice_in_dim(key_acc, key_part, key_start, 0)
        value_acc = lax.dynamic_update_slice_in_dim(value_acc, value_part, key_start, 0)
        return (query_acc, key_acc, value_acc)

    length_all = all_keys.shape[0]
    start_grads = (
        jnp.zeros((query_rows, head_width), jnp.float32),
        jnp.zeros((length_all, head_width), jnp.float32),
        jnp.zeros((length_all, head_width), jnp.float32),
    )
    grad_rot_query, key_sums, value_sums = lax.fori_loop(0, block_count, block_grads, start_grads)
    key_own, value_own = (
        lax.psum_scatter(
            key_sums.astype(jnp.bfloat16), ("ctx", "head"), scatter_dimension=0, tiled=True
        ).astype(jnp.float32),
        lax.psum_scatter(
            value_sums.astype(jnp.bfloat16), ("ctx", "head"), scatter_dimension=0, tiled=True
        ).astype(jnp.float32),
    )
    grad_rot_local = lax.all_to_all(
        grad_rot_query.reshape(query_rows, 1, head_width).astype(jnp.bfloat16),
        "head",
        split_axis=0,
        concat_axis=1,
        tiled=True,
    ).astype(jnp.float32)
    query_back = rotate(grad_rot_local * score_scale, cosine[:, None], -sine_part[:, None])
    grad_query_raw, gain_query = norm_back(query_raw, inverse_query, qk_gains[0], query_back)
    key_back = rotate(key_own, cosine, -sine_part)
    grad_key_raw, gain_key = norm_back(key_raw, inverse_key, qk_gains[1], key_back)
    grad_query_in = grad_query_raw.reshape(tok_rows, head_count * head_width).astype(jnp.bfloat16)
    grad_key_in = grad_key_raw.astype(jnp.bfloat16)
    grad_value_in = value_own.astype(jnp.bfloat16)
    group_count = lax.axis_size(("dp", "ctx"))
    inner_count = lax.axis_size("head")
    rows_all = (
        lax.all_gather(attn_in, "head", axis=0, tiled=True),
        lax.all_gather(mlp_in, "head", axis=0, tiled=True),
        lax.all_gather(grad_branch, "head", axis=0, tiled=True),
        lax.all_gather(grad_down_in, "head", axis=0, tiled=True),
    )
    cols_all = (
        lax.all_to_all(
            split_columns(grad_query_in, group_count, inner_count),
            "head",
            split_axis=2,
            concat_axis=0,
            tiled=True,
        ),
        lax.all_to_all(
            split_columns(grad_key_in, group_count, inner_count),
            "head",
            split_axis=2,
            concat_axis=0,
            tiled=True,
        ),
        lax.all_to_all(
            split_columns(grad_value_in, group_count, inner_count),
            "head",
            split_axis=2,
            concat_axis=0,
            tiled=True,
        ),
        lax.all_to_all(
            split_columns(grad_gate_in, group_count, inner_count),
            "head",
            split_axis=2,
            concat_axis=0,
            tiled=True,
        ),
        lax.all_to_all(
            split_columns(grad_up_in, group_count, inner_count),
            "head",
            split_axis=2,
            concat_axis=0,
            tiled=True,
        ),
        lax.all_to_all(
            split_columns(attn_out, group_count, inner_count),
            "head",
            split_axis=2,
            concat_axis=0,
            tiled=True,
        ),
        lax.all_to_all(
            split_columns(hidden, group_count, inner_count),
            "head",
            split_axis=2,
            concat_axis=0,
            tiled=True,
        ),
    )
    query_terms, key_terms, value_terms, gate_terms, up_terms, out_terms, down_terms = weight_terms(
        rows_all, cols_all, group_count
    )
    summed = (
        lax.psum_scatter(query_terms, ("dp", "ctx"), scatter_dimension=1, tiled=True),
        lax.psum_scatter(key_terms, ("dp", "ctx"), scatter_dimension=1, tiled=True),
        lax.psum_scatter(value_terms, ("dp", "ctx"), scatter_dimension=1, tiled=True),
        lax.psum_scatter(gate_terms, ("dp", "ctx"), scatter_dimension=1, tiled=True),
        lax.psum_scatter(up_terms, ("dp", "ctx"), scatter_dimension=1, tiled=True),
        lax.psum_scatter(out_terms, ("dp", "ctx"), scatter_dimension=0, tiled=True),
        lax.psum_scatter(down_terms, ("dp", "ctx"), scatter_dimension=0, tiled=True),
    )
    grad_query, grad_key, grad_value, grad_gate, grad_up, grad_out, grad_down = owned_slices(
        summed, model_width
    )
    grad_attn_in = jnp.einsum(
        "te,de->td", grad_query_in, full_query, preferred_element_type=jnp.float32
    )
    grad_attn_in = grad_attn_in + jnp.einsum(
        "te,de->td", grad_key_in, full_key, preferred_element_type=jnp.float32
    )
    grad_attn_in = grad_attn_in + jnp.einsum(
        "te,de->td", grad_value_in, full_value, preferred_element_type=jnp.float32
    )
    grad_in_part, gain_zero = norm_back(input_wide, inverse_in, norm_gains[0], grad_attn_in)
    d_block_in = (grad_middle + grad_in_part).astype(jnp.bfloat16)
    gain_terms = jnp.stack(
        [
            jnp.sum(gain_zero, axis=0),
            jnp.sum(gain_one, axis=0),
            jnp.sum(gain_two, axis=0),
            jnp.sum(gain_three, axis=0),
        ]
    )
    qk_terms = jnp.stack([jnp.sum(gain_query, axis=(0, 1)), jnp.sum(gain_key, axis=0)])
    grad_norm_gains, grad_qk_gains = lax.psum((gain_terms, qk_terms), ("dp", "ctx", "head"))
    return (
        block_out,
        d_block_in,
        grad_norm_gains,
        grad_qk_gains,
        grad_query,
        grad_key,
        grad_value,
        grad_out,
        grad_gate,
        grad_up,
        grad_down,
    )


def solution(mesh):
    in_specs = (
        P(("dp", "ctx", "head"), None),
        P(("dp", "ctx", "head"), None),
        P(("dp", "ctx")),
        P(),
        P(),
        P(None, ("dp", "ctx", "head")),
        P(None, ("dp", "ctx", "head")),
        P(None, ("dp", "ctx", "head")),
        P(("dp", "ctx", "head"), None),
        P(None, ("dp", "ctx", "head")),
        P(None, ("dp", "ctx", "head")),
        P(("dp", "ctx", "head"), None),
    )
    out_specs = (
        P(("dp", "ctx", "head"), None),
        P(("dp", "ctx", "head"), None),
        P(),
        P(),
        P(None, ("dp", "ctx", "head")),
        P(None, ("dp", "ctx", "head")),
        P(None, ("dp", "ctx", "head")),
        P(("dp", "ctx", "head"), None),
        P(None, ("dp", "ctx", "head")),
        P(None, ("dp", "ctx", "head")),
        P(("dp", "ctx", "head"), None),
    )
    return jax.shard_map(local, mesh=mesh, in_specs=in_specs, out_specs=out_specs, check_vma=False)
```

profile of v0, /device:TPU:0, one launch (start us, length us, event | category | flops | bytes accessed | tf_op | source)
XLA Modules:
  0.0 863.2 jit_solution(17192437228534337498)
XLA Ops:
  10.6 1.5 slice_reduce_fusion
  12.1 1.0 fusion.70
  13.7 44.5 %all_gather.39 = bf16[640,256]{0,1:T(8,128)(2,1)S(1)} all-gather(bf16[640,8]{0,1:T(8,128)(2,1)} %param.24), channel_id=1, replica_groups=mesh['dp'=4,'ctx'=2,'head'=4] {'dp','ctx','head'}, dimensions={1}, use_global_device_ids=true | all-gather | bytes 337920 | tf_op jit(solution)/shard_map/all_gather | solution.py:106
  59.0 1.0 fusion.72
  62.2 8.7 %all_gather.40 = bf16[1024,256]{1,0:T(8,128)(2,1)S(1)} all-gather(bf16[128,256]{1,0:T(8,128)(2,1)S(1)} %pad_maximum_fusion.2), channel_id=1, replica_groups=mesh['dp'=4,'ctx'=2,'head'=4] {'ctx','head'}, dimensions={0}, use_global_device_ids=true | all-gather | bytes 589824 | tf_op jit(solution)/shard_map/all_gather | solution.py:131
  70.9 38.9 %all_gather.42 = bf16[640,256]{0,1:T(8,128)(2,1)S(1)} all-gather(bf16[640,8]{0,1:T(8,128)(2,1)S(1)} %copy-done.47), channel_id=1, replica_groups=mesh['dp'=4,'ctx'=2,'head'=4] {'dp','ctx','head'}, dimensions={1}, use_global_device_ids=true | all-gather | bytes 337920 | tf_op jit(solution)/shard_map/all_gather | solution.py:107
  110.8 9.2 %all_gather.43 = bf16[1024,256]{1,0:T(8,128)(2,1)S(1)} all-gather(bf16[128,256]{1,0:T(8,128)(2,1)S(1)} %convolution_convert_fusion.1), channel_id=1, replica_groups=mesh['dp'=4,'ctx'=2,'head'=4] {'ctx','head'}, dimensions={0}, use_global_device_ids=true | all-gather | bytes 589824 | tf_op jit(solution)/shard_map/all_gather | solution.py:132
  120.0 1.9 fusion.102
  124.0 3.4 all-to-all-start
  127.4 5.9 all-to-all-done
  137.2 8.4 all_to_all.159
  146.6 1.1 copy.219
  147.8 1.9 multiply_reduce_fusion.9
  150.7 34.1 %all-gather.10.cloned.1.call-done = bf16[640,2048]{0,1:T(8,128)(2,1)} async-done(((bf16[640,64]{0,1:T(8,128)(2,1)}), bf16[640,2048]{0,1:T(8,128)(2,1)}) %all-gather.10.cloned.1.call-update) | async-done | bytes 2621456 | tf_op jit(solution)/shard_map/all_gather | solution.py:186
  184.8 3.8 fusion.103
  188.6 55.4 %all-gather.12.cloned.1.call-done = bf16[640,2048]{0,1:T(8,128)(2,1)} async-done(((bf16[640,64]{0,1:T(8,128)(2,1)}), bf16[640,2048]{0,1:T(8,128)(2,1)}) %all-gather.12.cloned.1.call-update) | async-done | bytes 2621456 | tf_op jit(solution)/shard_map/all_gather | solution.py:187
  244.0 4.2 multiply_convert_fusion.1
  248.2 55.0 %all-gather.14.cloned.1.call-done = bf16[2048,640]{1,0:T(8,128)(2,1)} async-done(((bf16[64,640]{1,0:T(8,128)(2,1)}), bf16[2048,640]{1,0:T(8,128)(2,1)}) %all-gather.14.cloned.1.call-update) | async-done | bytes 2621456 | tf_op jit(solution)/shard_map/all_gather | solution.py:188
  303.3 2.7 multiply_reduce_fusion.7
  306.0 1.7 fusion.69
  308.5 1.4 multiply_convert_fusion
  310.9 1.2 copy-done.1
  312.1 1.2 multiply_reduce_fusion.3
  316.3 3.4 all-to-all-start.2
  319.8 5.9 all-to-all-done.2
  327.6 3.4 while.41
  327.6 1.2 fusion.185
  331.1 7.3 all_gather.48
  339.1 4.0 all-to-all-start.7
  343.2 1.0 copy.248
  346.0 3.3 all-to-all-done.7
  349.2 1.2 copy.238
  351.2 8.6 all_gather.49
  360.5 1.8 reduce.11
  363.1 3.4 all-to-all-start.3
  366.6 2.2 fusion.51
  368.9 3.6 all-to-all-done.3
  375.7 3.5 all-to-all-start.5
  380.6 0.9 copy.283
  381.5 23.4 %reduce-scatter.28.cloned.1.call-done = bf16[128,256]{1,0:T(8,128)(2,1)} async-done(((bf16[1024,256]{1,0:T(8,128)(2,1)}), bf16[128,256]{1,0:T(8,128)(2,1)}) %reduce-scatter.28.cloned.1.call-update) | async-done | bytes 65552
  404.9 0.9 copy.249
  406.5 3.3 all-to-all-start.6
  409.8 0.9 convolution_bitcast_fusion.4
  410.8 1.5 multiply_reduce_fusion
  413.9 3.4 all-to-all-start.4
  418.3 4.9 all-to-all-done.4
  423.5 1.2 fusion.80
  425.9 3.5 all-to-all-start.8
  429.4 13.1 %all_gather.50 = bf16[512,640]{1,0:T(8,128)(2,1)S(1)} all-gather(bf16[128,640]{1,0:T(8,128)(2,1)S(1)} %copy-done.14), channel_id=1, replica_groups=mesh['dp'=4,'ctx'=2,'head'=4] {'head'}, dimensions={0}, use_global_device_ids=true | all-gather | bytes 819200 | tf_op jit(solution)/shard_map/all_gather | solution.py:282
  442.9 1.7 fusion.56
  445.0 11.2 %all_to_all.160 = bf16[128,8,4,64]{0,3,1,2:T(8,128)(2,1)S(1)} all-to-all(bf16[128,8,4,64]{0,3,1,2:T(8,128)(2,1)S(1)} %copy.243), channel_id=1, replica_groups=mesh['dp'=4,'ctx'=2,'head'=4] {'head'}, dimensions={2} | all-to-all | bytes 1048576 | tf_op jit(solution)/shard_map/all_to_all | solution.py:315
  456.6 1.6 fusion.53
  459.4 3.5 all-to-all-start.10
  463.0 13.1 %all_gather.51 = bf16[512,640]{1,0:T(8,128)(2,1)S(1)} all-gather(bf16[128,640]{1,0:T(8,128)(2,1)S(1)} %copy-done.34), channel_id=1, replica_groups=mesh['dp'=4,'ctx'=2,'head'=4] {'head'}, dimensions={0}, use_global_device_ids=true | all-gather | bytes 819200 | tf_op jit(solution)/shard_map/all_gather | solution.py:284
  476.1 1.2 copy.247
  477.3 1.3 reshape.354
  478.6 1.6 fusion.49
  481.7 39.5 %all-reduce.2 = (f32[4,640]{1,0:T(4,128)}, f32[2,256]{1,0:T(2,128)}) all-reduce(f32[4,640]{1,0:T(4,128)S(1)} %pad_maximum_fusion.3, f32[2,256]{1,0:T(2,128)S(1)} %pad_maximum_fusion.4), channel_id=1, replica_groups=mesh['dp'=4,'ctx'=2,'head'=4] {'dp','ctx','head'}, use_global_device_ids=true, to_apply=%region_27.28 | all-reduce | flops 3072 | bytes 24576 | tf_op jit(solution)/shard_map/psum | solution.py:372
  522.0 7.5 reduce-scatter.30.cloned.1.call-done
  529.5 57.8 %reduce-scatter.32.cloned.1.call-done = f32[640,1,8]{0,2,1:T(8,128)} async-done(((f32[640,8,8]{0,2,1:T(8,128)}), f32[640,1,8]{0,2,1:T(8,128)}) %reduce-scatter.32.cloned.1.call-update) | async-done | bytes 20496
  587.3 65.7 %reduce-scatter.18.cloned.1.call-done = f32[640,1,32]{0,2,1:T(8,128)} async-done(((f32[640,8,32]{0,2,1:T(8,128)}), f32[640,1,32]{0,2,1:T(8,128)}) %reduce-scatter.18.cloned.1.call-update) | async-done | bytes 81936 | tf_op jit(solution)/shard_map/reduce_scatter | solution.py:341
  653.0 67.9 %reduce-scatter.22.cloned.1.call-done = f32[640,1,64]{0,2,1:T(8,128)} async-done(((f32[640,8,64]{0,2,1:T(8,128)}), f32[640,1,64]{0,2,1:T(8,128)}) %reduce-scatter.22.cloned.1.call-update) | async-done | bytes 163856 | tf_op jit(solution)/shard_map/reduce_scatter | solution.py:344
  720.9 68.0 %reduce-scatter.24.cloned.1.call-done = f32[640,1,64]{0,2,1:T(8,128)} async-done(((f32[640,8,64]{0,2,1:T(8,128)}), f32[640,1,64]{0,2,1:T(8,128)}) %reduce-scatter.24.cloned.1.call-update) | async-done | bytes 163856 | tf_op jit(solution)/shard_map/reduce_scatter | solution.py:345
  788.9 67.8 %reduce-scatter.26.cloned.1.call-done = f32[1,64,640]{2,1,0:T(8,128)} async-done(((f32[8,64,640]{2,1,0:T(8,128)}), f32[1,64,640]{2,1,0:T(8,128)}) %reduce-scatter.26.cloned.1.call-update) | async-done | bytes 163856 | tf_op jit(solution)/shard_map/reduce_scatter | solution.py:347
  (272 shorter events, 44.6 us)
Async XLA Ops:
  7.2 63.7 %copy-start.47 = (bf16[640,8]{0,1:T(8,128)(2,1)S(1)}, bf16[640,8]{0,1:T(8,128)(2,1)}, u32[]{:S(2)}) copy-start(bf16[640,8]{0,1:T(8,128)(2,1)} %param.25) | copy-start | bytes 30724
  7.2 112.8 %all-gather.6.cloned.1.call-start = ((), (), s32[]{:S(2)}) async-start(), calls=%async_computation.20 | async-start | bytes 1351680 | tf_op jit(solution)/shard_map/all_gather | solution.py:105
  7.9 139.8 %all-gather.8.cloned.1.call-start = ((), (), s32[]{:S(2)}) async-start(), calls=%async_computation.21 | async-start | bytes 1351680 | tf_op jit(solution)/shard_map/all_gather | solution.py:108
  8.7 176.1 %all-gather.10.cloned.1.call-start = ((), (), s32[]{:S(2)}) async-start(), calls=%async_computation.22 | async-start | bytes 2703360 | tf_op jit(solution)/shard_map/all_gather | solution.py:186
  9.4 234.6 %all-gather.12.cloned.1.call-start = ((), (), s32[]{:S(2)}) async-start(), calls=%async_computation.23 | async-start | bytes 2703360 | tf_op jit(solution)/shard_map/all_gather | solution.py:187
  10.0 293.3 %all-gather.14.cloned.1.call-start = ((), (), s32[]{:S(2)}) async-start(), calls=%async_computation.24 | async-start | bytes 2703360 | tf_op jit(solution)/shard_map/all_gather | solution.py:188
  10.6 111.3 %copy-start.53 = (f32[128]{0:T(128)}, f32[128]{0:T(128)S(1)}, u32[]{:S(2)}) copy-start(f32[128]{0:T(128)S(1)} %multiply_exponential_fusion) | copy-start | bytes 1540
  13.7 48.1 %copy-start.49 = (f32[128]{0:T(128)}, f32[128]{0:T(128)S(1)}, u32[]{:S(2)}) copy-start(f32[128]{0:T(128)S(1)} %get-tuple-element.364) | copy-start | bytes 1540
  59.0 2.8 copy-start.39
  59.0 64.0 %copy-start.44 = (f32[1,256]{1,0:T(1,128)}, f32[1,256]{1,0:T(1,128)S(1)}, u32[]{:S(2)}) copy-start(f32[1,256]{1,0:T(1,128)S(1)} %get-tuple-element.356) | copy-start | bytes 3076
  60.4 59.6 %copy-start.24 = (f32[128,256]{1,0:T(8,128)}, f32[128,256]{1,0:T(8,128)S(1)}, u32[]{:S(2)}) copy-start(f32[128,256]{1,0:T(8,128)S(1)} %get-tuple-element.374) | copy-start | bytes 393220
  61.8 60.4 %copy-start.55 = (f32[128]{0:T(128)}, f32[128]{0:T(128)S(1)}, u32[]{:S(2)}) copy-start(f32[128]{0:T(128)S(1)} %dynamic-slice_convert_fusion) | copy-start | bytes 1540
  121.9 5.5 copy-start.58
  124.0 9.4 %all-to-all-start = ((bf16[128,4,256]{2,0,1:T(8,128)(2,1)}), bf16[128,4,256]{2,0,1:T(8,128)(2,1)S(1)}, u32[]{:S(2)}, u32[]{:S(2)}) async-start(bf16[128,4,256]{2,0,1:T(8,128)(2,1)} %fusion.61), calls=%async_computation | async-start | bytes 524288 | tf_op jit(solution)/shard_map/all_to_all | solution.py:127
  137.1 12.6 %copy-start.6 = (bf16[128,640]{1,0:T(8,128)(2,1)S(1)}, bf16[128,640]{1,0:T(8,128)(2,1)}, u32[]{:S(2)}) copy-start(bf16[128,640]{1,0:T(8,128)(2,1)} %param.18) | copy-start | bytes 491524
  248.2 57.8 %copy-start.36 = (f32[640]{0:T(1024)S(1)}, f32[640]{0:T(1024)}, u32[]{:S(2)}) copy-start(f32[640]{0:T(1024)} %get-tuple-element.261) | copy-start | bytes 7684
  303.2 4.4 copy-start.29
  303.2 5.2 copy-start.5
  303.3 5.2 copy-start.13
  303.3 5.2 copy-start.32
  309.9 3.4 copy-start.17
  309.9 3.4 copy-start.26
  312.1 2.9 copy-start.2
  315.0 10.8 %copy-start.30 = (bf16[128,640]{1,0:T(8,128)(2,1)}, bf16[128,640]{1,0:T(8,128)(2,1)S(1)}, u32[]{:S(2)}) copy-start(bf16[128,640]{1,0:T(8,128)(2,1)S(1)} %subtract_convert_fusion.1) | copy-start | bytes 491524
  316.3 9.4 %all-to-all-start.2 = ((bf16[128,4,256]{2,0,1:T(8,128)(2,1)}), bf16[128,4,256]{2,0,1:T(8,128)(2,1)S(1)}, u32[]{:S(2)}, u32[]{:S(2)}) async-start(bf16[128,4,256]{2,0,1:T(8,128)(2,1)} %bitcast.217), calls=%async_computation.2 | async-start | bytes 524288 | tf_op jit(solution)/shard_map/all_to_all | solution.py:219
  319.7 53.7 %reduce-scatter.16.cloned.1.call-start = ((), (), s32[]{:S(2)}) async-start(), calls=%async_computation.25 | async-start | bytes 589824 | tf_op jit(solution)/shard_map/reduce_scatter | solution.py:257
  327.6 10.8 %copy-start.16 = (bf16[128,4,1,256]{0,3,1,2:T(8,128)(2,1)S(1)}, bf16[128,4,1,256]{0,3,1,2:T(8,128)(2,1)}, u32[]{:S(2)}) copy-start(bf16[128,4,1,256]{0,3,1,2:T(8,128)(2,1)} %copy-done.15) | copy-start | bytes 786436
  331.0 12.2 %copy-start.23 = (bf16[1024,256]{0,1:T(8,128)(2,1)S(1)}, bf16[1024,256]{0,1:T(8,128)(2,1)}, u32[]{:S(2)}) copy-start(bf16[1024,256]{0,1:T(8,128)(2,1)} %get-tuple-element.178) | copy-start | bytes 1572868
  331.0 13.2 %copy-start.45 = (f32[1,256]{1,0:T(1,128)S(1)}, f32[1,256]{1,0:T(1,128)}, u32[]{:S(2)}) copy-start(f32[1,256]{1,0:T(1,128)} %copy-done.44) | copy-start | bytes 3076
  331.0 13.3 %copy-start.38 = (f32[128,4]{0,1:T(4,128)S(1)}, f32[128,4]{0,1:T(4,128)}, u32[]{:S(2)}) copy-start(f32[128,4]{0,1:T(4,128)} %copy-done.37) | copy-start | bytes 6148
  331.1 13.7 %copy-start.48 = (f32[128,4]{0,1:T(4,128)S(1)}, f32[128,4]{0,1:T(4,128)}, u32[]{:S(2)}) copy-start(f32[128,4]{0,1:T(4,128)} %get-tuple-element.354) | copy-start | bytes 6148
  339.1 10.1 %all-to-all-start.7 = ((bf16[128,8,4,32]{0,3,1,2:T(8,128)(2,1)}), bf16[128,8,4,32]{0,3,1,2:T(8,128)(2,1)}, u32[]{:S(2)}, u32[]{:S(2)}) async-start(bf16[128,8,4,32]{0,3,1,2:T(8,128)(2,1)} %copy.237), calls=%async_computation.9 | async-start | bytes 524288 | tf_op jit(solution)/shard_map/all_to_all | solution.py:322
  343.2 61.7 %reduce-scatter.28.cloned.1.call-start = ((), (), s32[]{:S(2)}) async-start(), calls=%async_computation.31 | async-start | bytes 589824
  344.2 7.0 copy-start.31
  363.1 9.4 %all-to-all-start.3 = ((bf16[4,2,16384]{2,1,0:T(2,128)(2,1)}), bf16[4,2,16384]{2,1,0:T(2,128)(2,1)S(1)}, u32[]{:S(2)}, u32[]{:S(2)}) async-start(bf16[4,2,16384]{2,1,0:T(2,128)(2,1)} %reshape.381), calls=%async_computation.3 | async-start | bytes 524288 | tf_op jit(solution)/shard_map/all_to_all | solution.py:264
  366.5 7.7 copy-start.54
  366.5 7.7 copy-start.56
  366.6 8.1 copy-start.25
  366.6 8.0 copy-start.40
  366.6 8.0 copy-start.52
  366.6 8.2 copy-start.60
  366.6 155.4 %reduce-scatter.20.cloned.1.call-start = ((), (), s32[]{:S(2)}) async-start(), calls=%async_computation.27 | async-start | bytes 737280 | tf_op jit(solution)/shard_map/reduce_scatter | solution.py:346
  368.8 10.4 %copy-start.46 = (f32[1,256]{1,0:T(1,128)S(1)}, f32[1,256]{1,0:T(1,128)}, u32[]{:S(2)}) copy-start(f32[1,256]{1,0:T(1,128)} %copy-done.44) | copy-start | bytes 3076
  375.7 30.8 %all-to-all-start.5 = ((bf16[128,8,4,8]{0,3,1,2:T(8,128)(2,1)}), bf16[128,8,4,8]{0,3,1,2:T(8,128)(2,1)S(1)}, u32[]{:S(2)}, u32[]{:S(2)}) async-start(bf16[128,8,4,8]{0,3,1,2:T(8,128)(2,1)} %copy.232), calls=%async_computation.7 | async-start | bytes 131072 | tf_op jit(solution)/shard_map/all_to_all | solution.py:294
  379.3 31.5 %copy-start.28 = (f32[16,8,4,256]{3,1,2,0:T(8,128)S(1)}, f32[16,8,4,256]{3,1,2,0:T(8,128)}, u32[]{:S(2)}) copy-start(f32[16,8,4,256]{3,1,2,0:T(8,128)} %copy.282) | copy-start | bytes 1572868
  406.5 7.4 all-to-all-start.6
  409.8 119.7 %reduce-scatter.30.cloned.1.call-start = ((), (), s32[]{:S(2)}) async-start(), calls=%async_computation.32 | async-start | bytes 184320
  412.3 12.5 %copy-start.27 = (bf16[128,2048]{1,0:T(8,128)(2,1)S(1)}, bf16[128,2048]{1,0:T(8,128)(2,1)}, u32[]{:S(2)}) copy-start(bf16[128,2048]{1,0:T(8,128)(2,1)} %copy-done.26) | copy-start | bytes 1572868
  413.9 9.4 %all-to-all-start.4 = ((bf16[128,8,4,32]{0,3,1,2:T(8,128)(2,1)}), bf16[128,8,4,32]{0,3,1,2:T(8,128)(2,1)S(1)}, u32[]{:S(2)}, u32[]{:S(2)}) async-start(bf16[128,8,4,32]{0,3,1,2:T(8,128)(2,1)} %copy.229), calls=%async_computation.5 | async-start | bytes 524288 | tf_op jit(solution)/shard_map/all_to_all | solution.py:287
  417.3 170.0 %reduce-scatter.32.cloned.1.call-start = ((), (), s32[]{:S(2)}) async-start(), calls=%async_computation.33 | async-start | bytes 184320
  418.3 234.7 %reduce-scatter.18.cloned.1.call-start = ((), (), s32[]{:S(2)}) async-start(), calls=%async_computation.26 | async-start | bytes 737280 | tf_op jit(solution)/shard_map/reduce_scatter | solution.py:341
  423.5 5.9 copy-start.14
  425.9 16.6 %all-to-all-start.8 = ((bf16[128,8,4,64]{0,3,1,2:T(8,128)(2,1)}), bf16[128,8,4,64]{0,3,1,2:T(8,128)(2,1)S(1)}, u32[]{:S(2)}, u32[]{:S(2)}) async-start(bf16[128,8,4,64]{0,3,1,2:T(8,128)(2,1)} %copy.240), calls=%async_computation.11 | async-start | bytes 1048576 | tf_op jit(solution)/shard_map/all_to_all | solution.py:308
  429.3 291.5 %reduce-scatter.22.cloned.1.call-start = ((), (), s32[]{:S(2)}) async-start(), calls=%async_computation.28 | async-start | bytes 1474560 | tf_op jit(solution)/shard_map/reduce_scatter | solution.py:344
  444.6 344.2 %reduce-scatter.24.cloned.1.call-start = ((), (), s32[]{:S(2)}) async-start(), calls=%async_computation.29 | async-start | bytes 1474560 | tf_op jit(solution)/shard_map/reduce_scatter | solution.py:345
  458.3 4.7 copy-start.34
  459.4 16.6 %all-to-all-start.10 = ((bf16[128,8,4,64]{0,3,1,2:T(8,128)(2,1)}), bf16[128,8,4,64]{0,3,1,2:T(8,128)(2,1)S(1)}, u32[]{:S(2)}, u32[]{:S(2)}) async-start(bf16[128,8,4,64]{0,3,1,2:T(8,128)(2,1)} %copy.246), calls=%async_computation.15 | async-start | bytes 1048576 | tf_op jit(solution)/shard_map/all_to_all | solution.py:329
  462.9 393.8 %reduce-scatter.26.cloned.1.call-start = ((), (), s32[]{:S(2)}) async-start(), calls=%async_computation.30 | async-start | bytes 1474560 | tf_op jit(solution)/shard_map/reduce_scatter | solution.py:347
  477.3 3.1 copy-start.41
  477.3 3.1 copy-start.42
  477.3 3.1 copy-start.43
  477.3 3.1 copy-start.3
  480.3 40.9 %copy-start.12 = (f32[128,640]{1,0:T(8,128)S(1)}, f32[128,640]{1,0:T(8,128)}, u32[]{:S(2)}) copy-start(f32[128,640]{1,0:T(8,128)} %copy-done.11) | copy-start | bytes 983044
  480.3 40.9 %copy-start.59 = (f32[128]{0:T(128)S(1)}, f32[128]{0:T(128)}, u32[]{:S(2)}) copy-start(f32[128]{0:T(128)} %get-tuple-element.363) | copy-start | bytes 1540
  (20 other events, 26.8 us)
Sparse Core Ops, SparseCore 0:
  10.8 57.1 all-gather.5
  70.8 54.2 all-gather.7
  128.0 56.7 all-gather.9
  187.5 56.4 all-gather.11
  246.7 56.4 all-gather.13
  331.2 36.4 reduce-scatter.15
  370.7 34.0 reduce-scatter.27
  408.7 62.7 reduce-scatter.19
  475.3 54.1 reduce-scatter.29
  533.1 54.2 reduce-scatter.31
  591.2 61.7 reduce-scatter.17
  656.8 64.0 reduce-scatter.21
  724.8 63.9 reduce-scatter.23
  792.7 63.9 reduce-scatter.25
where the time goes:
time: 865 us; the launch traced here: 863 us
  waiting for transfers between devices  530 us (61%)
  blocking collectives  202 us (23%)
  matrix products  33.5 us (4%)
  starting transfers between devices  32 us (4%)
  local copies, waits for them, and re-layouts  30.6 us (4%)
  other arithmetic  19.2 us (2%)
  between operations  15 us (2%)
    unnamed x17, waiting for transfers between devices  91.9 us
    reduce_scatter x1, waiting for transfers between devices, local(): lax.psum_scatter(up_terms, ('dp', 'ctx'), scatter_dimension=1, tiled=True)  68 us
    reduce_scatter x1, waiting for transfers between devices, local(): lax.psum_scatter(gate_terms, ('dp', 'ctx'), scatter_dimension=1, tiled=True)  67.9 us
    reduce_scatter x1, waiting for transfers between devices, local(): lax.psum_scatter(down_terms, ('dp', 'ctx'), scatter_dimension=0, tiled=True)  67.8 us
    reduce_scatter x1, waiting for transfers between devices, local(): lax.psum_scatter(query_terms, ('dp', 'ctx'), scatter_dimension=1, tiled=T...  65.7 us
    all_gather x1, waiting for transfers between devices, local(): lax.all_gather(w_up, ('dp', 'ctx', 'head'), axis=1, tiled=True)  55.4 us
    all_gather x1, waiting for transfers between devices, local(): lax.all_gather(w_down, ('dp', 'ctx', 'head'), axis=0, tiled=True)  55 us
    all_gather x1, blocking collectives, local(): lax.all_gather(w_key, ('dp', 'ctx', 'head'), axis=1, tiled=True)  44.5 us
  transfers between devices with their start and end apart: 23, of which 16 were waited for; matrix products, arithmetic and copies ran while one was open for 7% of the time, Pallas kernels for 0%

commit v1 on v0

v1 whole, which is shorter than its diff:
```python
import math

import jax
import jax.numpy as jnp
from jax import lax
from jax.experimental import pallas as pl
from jax.experimental.pallas import tpu as pltpu
from jax.sharding import PartitionSpec as P

epsilon = 1e-06
rope_base = 1000000.0
score_scale = 0.0625
negative_fill = -1e30


def norm_rows(values, gain_vec):
    inverse = lax.rsqrt(jnp.mean(values * values, axis=-1, keepdims=True) + epsilon)
    return (values * inverse * gain_vec, inverse)


def norm_back(values, inverse, gain_vec, upstream):
    scaled = upstream * gain_vec
    inner_mean = jnp.mean(scaled * values, axis=-1, keepdims=True)
    return (
        inverse * scaled - values * (inverse * inverse * inverse) * inner_mean,
        upstream * values * inverse,
    )


def rope_angles(positions, full_width):
    ladder = jnp.arange(full_width // 2, dtype=jnp.float32)
    frequency = jnp.exp(ladder * (-2.0 / full_width) * math.log(rope_base))
    angles = positions.astype(jnp.float32)[:, None] * frequency[None, :]
    return (jnp.cos(angles), jnp.sin(angles))


def rotate(values, cosine, sine_part):
    middle = values.shape[-1] // 2
    first_half = values[..., :middle]
    second = values[..., middle:]
    return jnp.concatenate(
        [first_half * cosine - second * sine_part, second * cosine + first_half * sine_part],
        axis=-1,
    )


def gelu_product(gate_pre, up_pre):
    return jax.nn.gelu(gate_pre, approximate=True) * up_pre


every_axis = ("dp", "ctx", "head")
sequence_axes = ("ctx", "head")
weight_axes = ("dp", "ctx")


def place_in(axes):
    place = 0
    for name in axes:
        place = place * lax.axis_size(name) + lax.axis_index(name)
    return place


def coordinates(axes, place):
    found = {}
    for name in reversed(axes):
        size = lax.axis_size(name)
        found[name] = lax.rem(place, size)
        place = place // size
    return found


def each_peer(count, step):
    if count <= 8:
        for offset in range(1, count):
            step(offset)
    else:

        def looped(offset, carry):
            step(offset)
            return carry

        lax.fori_loop(1, count, looped, 0)


def exchange_kernel(kinds, greet, counts, *refs):
    total = len(kinds)
    sources, targets, sems = refs[:total], refs[total : 2 * total], refs[2 * total :]
    barrier = pltpu.get_barrier_semaphore()
    waits = 0
    for axes, count in greet:
        me = place_in(axes)

        def greet_peer(offset, axes=axes, count=count, me=me):
            pl.semaphore_signal(
                barrier,
                inc=1,
                device_id=coordinates(axes, lax.rem(me + offset, count)),
                device_id_type=pl.DeviceIdType.MESH,
            )

        each_peer(count, greet_peer)
        waits += count - 1
    locals_started = []
    for part, (kind, axes) in enumerate(kinds):
        me = place_in(axes)
        source = sources[part].at[me] if kind == "scatter" else sources[part]
        copy = pltpu.make_async_copy(source, targets[part].at[me], sems[3 * part + 2].at[0])
        copy.start()
        locals_started.append(copy)
    pl.semaphore_wait(barrier, waits)

    def descriptor(part, offset, backward):
        kind, axes = kinds[part]
        count = counts[part]
        me = place_in(axes)
        to = lax.rem(me + offset, count)
        origin = lax.rem(me + count - offset, count) if backward else me
        source = sources[part].at[to] if kind == "scatter" else sources[part]
        return pltpu.make_async_remote_copy(
            src_ref=source,
            dst_ref=targets[part].at[origin],
            send_sem=sems[3 * part].at[offset],
            recv_sem=sems[3 * part + 1].at[origin],
            device_id=coordinates(axes, to),
            device_id_type=pl.DeviceIdType.MESH,
        )

    for part in range(total):
        each_peer(counts[part], lambda offset: descriptor(part, offset, False).start())
    for copy in locals_started:
        copy.wait()
    for part in range(total):
        each_peer(counts[part], lambda offset: descriptor(part, offset, True).wait_recv())
    for part in range(total):
        each_peer(counts[part], lambda offset: descriptor(part, offset, False).wait_send())


def exchange(call_id, name, parts, greet_axes=None):
    kinds = tuple((kind, axes) for kind, axes, _ in parts)
    arrays = [array for _, _, array in parts]
    counts = tuple(lax.axis_size(axes) for _, axes in kinds)
    if greet_axes is None:
        greet_axes = kinds[0][1]
    greet = ((greet_axes, lax.axis_size(greet_axes)),)
    shapes = [
        jax.ShapeDtypeStruct(
            array.shape if kind == "scatter" else (count,) + array.shape, array.dtype
        )
        for (kind, _, array), count in zip(parts, counts)
    ]
    scratch = []
    for count in counts:
        scratch += [
            pltpu.SemaphoreType.DMA((count,)),
            pltpu.SemaphoreType.DMA((count,)),
            pltpu.SemaphoreType.DMA((1,)),
        ]
    in_vmem = pl.BlockSpec(memory_space=pltpu.VMEM)
    return pl.pallas_call(
        lambda *refs: exchange_kernel(kinds, greet, counts, *refs),
        out_shape=shapes,
        in_specs=[in_vmem] * len(arrays),
        out_specs=[in_vmem] * len(arrays),
        scratch_shapes=scratch,
        compiler_params=pltpu.CompilerParams(collective_id=call_id, has_side_effects=True),
        name=name,
    )(*arrays)


def rows_dot(left, right, left_dim, right_dim):
    return lax.dot_general(
        left, right, (((left_dim,), (right_dim,)), ((), ())), preferred_element_type=jnp.float32
    )


def add_up(blocks):
    return jnp.sum(blocks.astype(jnp.float32), axis=0)


def local(
    block_in,
    cotangent,
    positions,
    norm_gains,
    qk_gains,
    w_query,
    w_key,
    w_value,
    w_out,
    w_gate,
    w_up,
    w_down,
):
    tok_rows, model_width = block_in.shape
    head_count = lax.axis_size("head")
    head_width = qk_gains.shape[1]
    ctx_slot = lax.axis_index("ctx")
    query_rows = head_count * tok_rows
    group_count = lax.axis_size(weight_axes)
    every_count = lax.axis_size(every_axis)
    length_all = lax.axis_size(sequence_axes) * tok_rows
    query_cols = w_query.shape[1]
    key_cols = w_key.shape[1]
    ff_cols = w_gate.shape[1]
    narrow = jnp.bfloat16

    ff_rows = jnp.concatenate([w_gate.T, w_up.T, w_down], axis=0)
    ff_all = lax.all_gather(ff_rows, weight_axes, axis=0, tiled=False)

    to_heads = [
        (head * group_count + index, index * head_count + head)
        for head in range(head_count)
        for index in range(group_count)
    ]
    to_owners = [(there, here) for here, there in to_heads]
    head_rows = lax.ppermute(
        jnp.concatenate([w_query.T, w_out], axis=0), every_axis, to_heads
    )
    key_value_rows = jnp.concatenate([w_key.T, w_value.T], axis=0)
    block_all, key_value_all, head_all, position_all = exchange(
        1,
        "first_gather",
        [
            ("gather", sequence_axes, block_in),
            ("gather", every_axis, key_value_rows),
            ("gather", weight_axes, head_rows),
            ("gather", ("ctx",), positions.reshape(-1, 128)),
        ],
        every_axis,
    )
    query_weight = head_all[:, :query_cols].reshape(head_width, model_width)
    out_weight = head_all[:, query_cols:].reshape(head_width, model_width)
    key_weight = key_value_all[:, :key_cols].reshape(head_width, model_width)
    value_weight = key_value_all[:, key_cols:].reshape(head_width, model_width)

    input_all = block_all.reshape(length_all, model_width).astype(jnp.float32)
    attn_in_all = norm_rows(input_all, norm_gains[0])[0].astype(narrow)
    first_query = ctx_slot * query_rows
    attn_in = lax.dynamic_slice_in_dim(attn_in_all, first_query, query_rows)
    query_raw = rows_dot(attn_in, query_weight, 1, 1)
    key_raw = rows_dot(attn_in_all, key_weight, 1, 1)
    all_values = rows_dot(attn_in_all, value_weight, 1, 1).astype(narrow)
    query_normed, inverse_query = norm_rows(query_raw, qk_gains[0])
    key_normed, inverse_key = norm_rows(key_raw, qk_gains[1])
    cosine, sine_part = rope_angles(position_all.reshape(length_all), head_width)
    cosine_own = lax.dynamic_slice_in_dim(cosine, first_query, query_rows)
    sine_own = lax.dynamic_slice_in_dim(sine_part, first_query, query_rows)
    head_query = (rotate(query_normed, cosine_own, sine_own) * score_scale).astype(narrow)
    all_keys = rotate(key_normed, cosine, sine_part).astype(narrow)

    query_index = first_query + jnp.arange(query_rows, dtype=jnp.int32)
    lowest_key = query_index - positions
    key_index = jnp.arange(length_all, dtype=jnp.int32)
    visible = (key_index[None, :] <= query_index[:, None]) & (
        key_index[None, :] >= lowest_key[:, None]
    )
    scores = jnp.where(visible, rows_dot(head_query, all_keys, 1, 1), negative_fill)
    top = jnp.max(scores, axis=1, keepdims=True)
    log_total = top + jnp.log(jnp.sum(jnp.exp(scores - top), axis=1, keepdims=True))
    probs_wide = jnp.exp(scores - log_total)
    prob_rows = probs_wide.astype(narrow)
    attn_exact = rows_dot(prob_rows, all_values, 1, 0)
    attn_out = attn_exact.astype(narrow)
    branch_part = rows_dot(attn_out, out_weight, 1, 0).astype(narrow)
    (branch_blocks,) = exchange(
        2,
        "branch_scatter",
        [("scatter", ("head",), branch_part.reshape(head_count, tok_rows, model_width))],
    )
    branch = add_up(branch_blocks)
    input_wide = block_in.astype(jnp.float32)
    inverse_in = norm_rows(input_wide, norm_gains[0])[1]
    branch_normed, inverse_branch = norm_rows(branch, norm_gains[1])
    middle = input_wide + branch_normed
    mlp_norm, inverse_mid = norm_rows(middle, norm_gains[2])
    (mlp_blocks,) = exchange(
        3, "mlp_gather", [("gather", ("head",), mlp_norm.astype(narrow))]
    )
    mlp_in = mlp_blocks.reshape(query_rows, model_width)

    ff_width = group_count * ff_cols
    gate_weight = ff_all[:, :ff_cols].reshape(ff_width, model_width)
    up_weight = ff_all[:, ff_cols : 2 * ff_cols].reshape(ff_width, model_width)
    down_weight = ff_all[:, 2 * ff_cols :].reshape(ff_width, model_width)
    gate_pre = rows_dot(mlp_in, gate_weight, 1, 1)
    up_pre = rows_dot(mlp_in, up_weight, 1, 1)
    hidden = gelu_product(gate_pre, up_pre).astype(narrow)
    down_part = rows_dot(hidden, down_weight, 1, 0).astype(narrow)
    (down_blocks,) = exchange(
        4,
        "down_scatter",
        [("scatter", ("head",), down_part.reshape(head_count, tok_rows, model_width))],
    )
    down_raw = add_up(down_blocks)
    down_normed, inverse_down = norm_rows(down_raw, norm_gains[3])
    block_out = (middle + down_normed).astype(narrow)
    cot_wide = cotangent.astype(jnp.float32)
    grad_down_raw, gain_three = norm_back(down_raw, inverse_down, norm_gains[3], cot_wide)
    (grad_down_blocks,) = exchange(
        5, "grad_down_gather", [("gather", ("head",), grad_down_raw.astype(narrow))]
    )
    grad_down_in = grad_down_blocks.reshape(query_rows, model_width)
    grad_hidden = rows_dot(grad_down_in, down_weight, 1, 1)
    _, gelu_pull = jax.vjp(gelu_product, gate_pre, up_pre)
    grad_gate_raw, grad_up_raw = gelu_pull(grad_hidden)
    grad_gate_in = grad_gate_raw.astype(narrow)
    grad_up_in = grad_up_raw.astype(narrow)
    grad_mlp_part = rows_dot(grad_gate_in, gate_weight, 1, 0) + rows_dot(
        grad_up_in, up_weight, 1, 0
    )
    (grad_mlp_blocks,) = exchange(
        6,
        "grad_mlp_scatter",
        [
            (
                "scatter",
                ("head",),
                grad_mlp_part.astype(narrow).reshape(head_count, tok_rows, model_width),
            )
        ],
    )
    ff_terms = jnp.concatenate(
        [
            rows_dot(grad_gate_in, mlp_in, 0, 0).reshape(group_count, ff_cols, model_width),
            rows_dot(grad_up_in, mlp_in, 0, 0).reshape(group_count, ff_cols, model_width),
            rows_dot(hidden, grad_down_in, 0, 0).reshape(group_count, ff_cols, model_width),
        ],
        axis=1,
    ).astype(narrow)
    ff_blocks = lax.all_to_all(ff_terms, weight_axes, split_axis=0, concat_axis=0, tiled=True)

    grad_mlp_in = add_up(grad_mlp_blocks)
    grad_mid_part, gain_two = norm_back(middle, inverse_mid, norm_gains[2], grad_mlp_in)
    grad_middle = cot_wide + grad_mid_part
    grad_branch_raw, gain_one = norm_back(branch, inverse_branch, norm_gains[1], grad_middle)
    (grad_branch_blocks,) = exchange(
        7, "grad_branch_gather", [("gather", ("head",), grad_branch_raw.astype(narrow))]
    )
    grad_branch = grad_branch_blocks.reshape(query_rows, model_width)
    head_grad = rows_dot(grad_branch, out_weight, 1, 1).astype(narrow)
    row_delta = jnp.sum(head_grad.astype(jnp.float32) * attn_exact, axis=1, keepdims=True)
    grad_probs = rows_dot(head_grad, all_values, 1, 1)
    grad_scores = (probs_wide * (grad_probs - row_delta)).astype(narrow)
    value_sums = rows_dot(prob_rows, head_grad, 0, 0)
    key_sums = rows_dot(grad_scores, head_query, 0, 0)
    grad_rot_query = rows_dot(grad_scores, all_keys, 1, 0)
    query_back = rotate(grad_rot_query * score_scale, cosine_own, -sine_own)
    grad_query_raw, gain_query = norm_back(query_raw, inverse_query, qk_gains[0], query_back)
    key_back = rotate(key_sums, cosine, -sine_part)
    grad_key_raw, gain_key = norm_back(key_raw, inverse_key, qk_gains[1], key_back)
    grad_query_in = grad_query_raw.astype(narrow)
    grad_key_in = grad_key_raw.astype(narrow)
    grad_value_in = value_sums.astype(narrow)
    grad_attn_part = rows_dot(grad_key_in, key_weight, 1, 0) + rows_dot(
        grad_value_in, value_weight, 1, 0
    )
    own_part = lax.dynamic_slice_in_dim(grad_attn_part, first_query, query_rows) + rows_dot(
        grad_query_in, query_weight, 1, 0
    )
    grad_attn_part = lax.dynamic_update_slice_in_dim(grad_attn_part, own_part, first_query, 0)
    head_terms = jnp.concatenate(
        [
            rows_dot(grad_query_in, attn_in, 0, 0).reshape(group_count, query_cols, model_width),
            rows_dot(attn_out, grad_branch, 0, 0).reshape(group_count, query_cols, model_width),
        ],
        axis=1,
    ).astype(narrow)
    key_value_terms = jnp.concatenate(
        [
            rows_dot(grad_key_in, attn_in_all, 0, 0).reshape(every_count, key_cols, model_width),
            rows_dot(grad_value_in, attn_in_all, 0, 0).reshape(every_count, key_cols, model_width),
        ],
        axis=1,
    ).astype(narrow)
    grad_attn_blocks, head_blocks, key_value_blocks = exchange(
        8,
        "last_scatter",
        [
            (
                "scatter",
                sequence_axes,
                grad_attn_part.astype(narrow).reshape(-1, tok_rows, model_width),
            ),
            ("scatter", weight_axes, head_terms),
            ("scatter", every_axis, key_value_terms),
        ],
        every_axis,
    )
    grad_attn_in = add_up(grad_attn_blocks)
    grad_in_part, gain_zero = norm_back(input_wide, inverse_in, norm_gains[0], grad_attn_in)
    d_block_in = (grad_middle + grad_in_part).astype(narrow)

    pad = ((0, 0), (0, model_width - head_width))
    gain_terms = jnp.concatenate(
        [
            jnp.sum(gain_zero, axis=0, keepdims=True),
            jnp.sum(gain_one, axis=0, keepdims=True),
            jnp.sum(gain_two, axis=0, keepdims=True),
            jnp.sum(gain_three, axis=0, keepdims=True),
            jnp.pad(jnp.sum(gain_query, axis=0, keepdims=True), pad),
            jnp.pad(jnp.sum(gain_key, axis=0, keepdims=True), pad),
            jnp.zeros((2, model_width), jnp.float32),
        ],
        axis=0,
    )
    (gain_blocks,) = exchange(9, "gain_gather", [("gather", every_axis, gain_terms)])
    gains = add_up(gain_blocks)

    head_own = lax.ppermute(add_up(head_blocks).astype(narrow), every_axis, to_owners).astype(
        jnp.float32
    )
    key_value_own = add_up(key_value_blocks)
    ff_own = add_up(ff_blocks)
    return (
        block_out,
        d_block_in,
        gains[:4],
        gains[4:6, :head_width],
        head_own[:query_cols].T,
        key_value_own[:key_cols].T,
        key_value_own[key_cols:].T,
        head_own[query_cols:],
        ff_own[:ff_cols].T,
        ff_own[ff_cols : 2 * ff_cols].T,
        ff_own[2 * ff_cols :],
    )


def solution(mesh):
    in_specs = (
        P(("dp", "ctx", "head"), None),
        P(("dp", "ctx", "head"), None),
        P(("dp", "ctx")),
        P(),
        P(),
        P(None, ("dp", "ctx", "head")),
        P(None, ("dp", "ctx", "head")),
        P(None, ("dp", "ctx", "head")),
        P(("dp", "ctx", "head"), None),
        P(None, ("dp", "ctx", "head")),
        P(None, ("dp", "ctx", "head")),
        P(("dp", "ctx", "head"), None),
    )
    out_specs = (
        P(("dp", "ctx", "head"), None),
        P(("dp", "ctx", "head"), None),
        P(),
        P(),
        P(None, ("dp", "ctx", "head")),
        P(None, ("dp", "ctx", "head")),
        P(None, ("dp", "ctx", "head")),
        P(("dp", "ctx", "head"), None),
        P(None, ("dp", "ctx", "head")),
        P(None, ("dp", "ctx", "head")),
        P(("dp", "ctx", "head"), None),
    )
    return jax.shard_map(local, mesh=mesh, in_specs=in_specs, out_specs=out_specs, check_vma=False)
```

time: 865 us -> 337 us (0.39)
  waiting for transfers between devices: 530 us -> 0.04 us
  Pallas kernels: 0 us -> 209 us
  blocking collectives: 202 us -> 0 us
  other arithmetic: 19.2 us -> 36 us
  starting transfers between devices: 32 us -> 15.2 us
    reduce_scatter x6 -> x0, waiting for transfers between devices: 269 us -> none  [the longest x1 68 us: local(): lax.psum_scatter(up_terms, ('dp', 'ctx'), scatter_dimension=1, tiled=True)]
    pallas_call x0 -> x9, Pallas kernels: none -> 209 us  [exchange(): pl.pallas_call(lambda *refs: exchange_kernel(kinds, greet, counts, *refs)...]
    all_gather x5 -> x1, waiting for transfers between devices: 145 us -> 0.02 us  [local(): ff_all = lax.all_gather(ff_rows, weight_axes, axis=0, tiled=False)]
    all_gather x8 -> x0, blocking collectives: 143 us -> none  [the longest x1 44.5 us: local(): lax.all_gather(w_key, ('dp', 'ctx', 'head'), axis=1, tiled=True)]
    unnamed x17 -> x1, waiting for transfers between devices: 91.9 us -> 0.02 us
    psum x1 -> x0, blocking collectives: 39.5 us -> none  [local(): lax.psum((gain_terms, qk_terms), ('dp', 'ctx', 'head'))]
    all_to_all x9 -> x1, waiting for transfers between devices: 24.4 us -> 0.01 us  [local(): lax.all_to_all(ff_terms, weight_axes, split_axis=0, concat_axis=0, tiled=...]
    all_to_all x2 -> x0, blocking collectives: 19.6 us -> none  [the longest x1 11.2 us: local(): lax.all_to_all(split_columns(grad_up_in, group_count, inner_count), 'head...]
  transfers between devices with their start and end apart: 23 -> 4, of which waited for: 16 -> 0; matrix products, arithmetic and copies ran while one was open for 7% -> 10% of each run, Pallas kernels for 0% -> 49%
where the time goes in v1:
time: 337 us; the launch traced here: 332 us
  Pallas kernels  209 us (62%)
  other arithmetic  36 us (11%)
  matrix products  32.2 us (10%)
  local copies, waits for them, and re-layouts  24.4 us (7%)
  starting transfers between devices  15.2 us (5%)
  between operations  15 us (4%)
    pallas_call x9, Pallas kernels, exchange(): pl.pallas_call(lambda *refs: exchange_kernel(kinds, greet, counts, *refs)...  209 us
    dot_general x27, matrix products, rows_dot(): lax.dot_general(left, right, (((left_dim,), (right_dim,)), ((), ())), pre...  32.2 us
    all_to_all x1, starting transfers between devices, local(): lax.all_to_all(ff_terms, weight_axes, split_axis=0, concat_axis=0, tiled=...  13.8 us
    reduce_sum x8, other arithmetic, add_up(): return jnp.sum(blocks.astype(jnp.float32), axis=0)  9.52 us
    dot_general x3, local copies, waits for them, and re-layouts, rows_dot(): lax.dot_general(left, right, (((left_dim,), (right_dim,)), ((), ())), pre...  7.65 us
    unnamed x110, local copies, waits for them, and re-layouts  7.62 us
  transfers between devices with their start and end apart: 4, of which 0 were waited for; matrix products, arithmetic and copies ran while one was open for 10% of the time, Pallas kernels for 49%

profile of v1, /device:TPU:0, one launch (start us, length us, event | category | flops | bytes accessed | tf_op | source)
XLA Modules:
  0.0 332.2 jit_solution(16068365829052101274)
XLA Ops:
  7.2 1.7 pad_maximum_fusion.8
  8.9 0.8 pad_maximum_fusion.9
  9.7 0.7 collective-permute-start
  10.4 0.9 slice_reduce_fusion
  11.3 0.8 fusion.104
  12.0 0.7 iota_add_fusion
  12.7 1.3 pad_maximum_fusion.10.refs_1_
  14.1 0.6 copy-done.50
  14.7 53.9 %first_gather.1 = (bf16[8,128,640]{2,1,0:T(8,128)(2,1)}, bf16[32,16,640]{2,1,0:T(8,128)(2,1)}, bf16[8,64,640]{2,1,0:T(8,128)(2,1)}, s32[2,4,128]{2,1,0:T(4,128)}) custom-call(bf16[128,640]{1,0:T(8,128)(2,1)} %refs_0_.1, bf16[16,640]{1,0:T(8,128)(2,1)} %pad_maximum_fusion.10.refs_1_, bf16[64,640]{1,0:T(8,128)(2,1)} %copy-done.50, s32[4,128]{1,0:T(4,128)} %bitcast.189), custom_call_target="tpu_custom_call" | custom-call | tf_op jit(solution)/shard_map/first_gather/pallas_call | solution.py:159
  68.6 1.7 multiply_reduce_fusion
  71.4 0.8 copy-done.40
  74.2 2.1 multiply_cosine_fusion
  76.6 0.8 fusion.105
  78.8 1.4 fusion.106
  80.3 1.3 convolution_convert_fusion
  81.6 11.8 %branch_scatter.1 = bf16[4,128,640]{2,1,0:T(8,128)(2,1)} custom-call(bf16[4,128,640]{2,1,0:T(8,128)(2,1)} %bitcast.161), custom_call_target="tpu_custom_call" | custom-call | tf_op jit(solution)/shard_map/branch_scatter/pallas_call | solution.py:159
  93.4 1.2 convert_reduce_fusion.5
  95.0 0.8 multiply_convert_fusion.6.refs_0_
  95.7 11.3 %mlp_gather.1 = bf16[4,128,640]{2,1,0:T(8,128)(2,1)} custom-call(bf16[128,640]{1,0:T(8,128)(2,1)} %multiply_convert_fusion.6.refs_0_), custom_call_target="tpu_custom_call" | custom-call | tf_op jit(solution)/shard_map/mlp_gather/pallas_call | solution.py:159
  107.1 2.8 fusion.101
  109.9 0.8 copy-done.8
  110.7 1.6 fusion.108
  112.4 2.6 copy.28
  114.9 2.9 fusion.107
  117.8 2.5 copy.27
  120.3 3.4 %convolution_convert_fusion.4 = bf16[512,640]{1,0:T(8,128)(2,1)} fusion(bf16[512,640]{1,0:T(8,128)(2,1)} %bitcast.174, f32[512,512]{1,0:T(8,128)} %copy.28, f32[512,512]{1,0:T(8,128)} %copy.27), kind=kOutput, calls=%fused_computation.26 | convolution fusion | flops 338493440 | bytes 3407872 | tf_op jit(solution)/shard_map/dot_general | solution.py:171
  123.7 11.5 %down_scatter.1 = bf16[4,128,640]{2,1,0:T(8,128)(2,1)} custom-call(bf16[4,128,640]{2,1,0:T(8,128)(2,1)} %bitcast.173), custom_call_target="tpu_custom_call" | custom-call | tf_op jit(solution)/shard_map/down_scatter/pallas_call | solution.py:159
  135.2 1.2 convert_reduce_fusion.4
  136.5 1.1 fusion.51
  137.6 1.8 fusion.48
  139.4 11.3 %grad_down_gather.1 = bf16[4,128,640]{2,1,0:T(8,128)(2,1)} custom-call(bf16[128,640]{1,0:T(8,128)(2,1)} %get-tuple-element.63.refs_0_), custom_call_target="tpu_custom_call" | custom-call | tf_op jit(solution)/shard_map/grad_down_gather/pallas_call | solution.py:159
  150.7 4.7 %fusion.20 = (bf16[512,512]{1,0:T(8,128)(2,1)}, bf16[512,512]{1,0:T(8,128)(2,1)}, bf16[512,512]{1,0:T(8,128)(2,1)}, f32[512,512]{0,1:T(8,128)}) fusion(f32[512,512]{0,1:T(8,128)} %fusion.107, f32[512,512]{0,1:T(8,128)} %fusion.108, bf16[512,640]{1,0:T(8,128)(2,1)} %bitcast.171, bf16[512,640]{1,0:T(8,128)(2,1)} %bitcast.175), kind=kOutput, calls=%fused_computation.55 | convolution fusion | flops 342360064 | bytes 6029312 | tf_op jit(solution)/shard_map/dot_general | solution.py:171
  155.4 2.6 copy.29
  158.0 3.4 %fusion.43 = f32[512,640]{1,0:T(8,128)S(1)} fusion(bf16[512,640]{1,0:T(8,128)(2,1)} %bitcast.163, f32[512,512]{1,0:T(8,128)} %copy.27, f32[512,512]{1,0:T(8,128)} %copy.29, f32[512,512]{1,0:T(8,128)} %copy.28), kind=kOutput, calls=%fused_computation.110 | convolution fusion | flops 341049344 | bytes 5111808 | tf_op jit(solution)/shard_map/dot_general | solution.py:171
  161.4 1.7 fusion.4
  163.0 11.4 %grad_mlp_scatter.1 = bf16[4,128,640]{2,1,0:T(8,128)(2,1)} custom-call(bf16[4,128,640]{2,1,0:T(8,128)(2,1)} %bitcast.160), custom_call_target="tpu_custom_call" | custom-call | tf_op jit(solution)/shard_map/grad_mlp_scatter/pallas_call | solution.py:159
  174.5 1.2 convert_reduce_fusion.3
  175.9 1.2 multiply_reduce_fusion.9
  177.1 0.7 copy-done.17
  177.8 0.8 subtract_convert_fusion.2.refs_0_
  178.6 11.3 %grad_branch_gather.1 = bf16[4,128,640]{2,1,0:T(8,128)(2,1)} custom-call(bf16[128,640]{1,0:T(8,128)(2,1)} %subtract_convert_fusion.2.refs_0_), custom_call_target="tpu_custom_call" | custom-call | tf_op jit(solution)/shard_map/grad_branch_gather/pallas_call | solution.py:159
  189.9 1.8 multiply_reduce_fusion.6
  192.3 0.7 multiply_convert_fusion.1
  195.7 2.1 fusion.34
  198.8 0.6 copy-done.6
  201.4 1.5 pad_maximum_fusion
  202.9 13.8 %all-to-all-start = ((bf16[8,192,640]{2,1,0:T(8,128)(2,1)}), bf16[8,192,640]{2,1,0:T(8,128)(2,1)}, u32[]{:S(2)}, u32[]{:S(2)}) async-start(bf16[8,192,640]{2,1,0:T(8,128)(2,1)} %pad_maximum_fusion), calls=%async_computation | async-start | bytes 3932160 | tf_op jit(solution)/shard_map/all_to_all | solution.py:330
  216.7 1.8 subtract_convert_fusion
  220.2 1.3 convert_element_type.186
  221.5 0.9 copy-done.2
  223.2 0.9 pad_maximum_fusion.2.refs_1_
  225.3 0.9 pad_maximum_fusion.3.refs_2_
  226.2 63.0 %last_scatter.1 = (bf16[8,128,640]{2,1,0:T(8,128)(2,1)}, bf16[8,64,640]{2,1,0:T(8,128)(2,1)}, bf16[32,16,640]{2,1,0:T(8,128)(2,1)}) custom-call(bf16[8,128,640]{2,1,0:T(8,128)(2,1)} %bitcast.155, bf16[8,64,640]{2,1,0:T(8,128)(2,1)} %pad_maximum_fusion.2.refs_1_, bf16[32,16,640]{2,1,0:T(8,128)(2,1)} %pad_maximum_fusion.3.refs_2_), custom_call_target="tpu_custom_call" | custom-call | tf_op jit(solution)/shard_map/last_scatter/pallas_call | solution.py:159
  289.3 1.3 reduce_sum.290
  290.6 0.7 collective-permute-start.1
  291.2 1.5 convert_reduce_fusion.1
  293.0 0.8 fusion.56
  294.5 0.6 concatenate.46.refs_0_
  295.2 23.9 %gain_gather.1 = f32[32,8,640]{2,1,0:T(8,128)} custom-call(f32[8,640]{1,0:T(8,128)} %concatenate.46.refs_0_), custom_call_target="tpu_custom_call" | custom-call | tf_op jit(solution)/shard_map/gain_gather/pallas_call | solution.py:159
  319.1 1.1 reduce_sum.289
  321.4 0.6 slice.142
  322.1 0.6 slice_bitcast_fusion.2
  322.7 1.9 convert_reduce_fusion
  324.6 0.8 fusion.103
  (171 shorter events, 16.9 us)
Async XLA Ops:
  7.2 99.9 %all-gather.3.cloned.1.call-start = ((), (), s32[]{:S(2)}) async-start(), calls=%async_computation.1 | async-start | bytes 2211840 | tf_op jit(solution)/shard_map/all_gather | solution.py:208
  9.7 4.3 %collective-permute-start = (bf16[64,640]{1,0:T(8,128)(2,1)S(1)}, bf16[64,640]{1,0:T(8,128)(2,1)S(1)}, u32[]{:S(2)}, u32[]{:S(2)}) collective-permute-start(bf16[64,640]{1,0:T(8,128)(2,1)S(1)} %pad_maximum_fusion.9), channel_id=1, source_target_pairs={{0,0},{1,4},{2,8},{3,12},{4,16},{5,20},{6,24},{7,28},{8,1},{9,5},{... | collective-permute-start | bytes 245768 | tf_op jit(solution)/shard_map/ppermute | solution.py:216
  14.1 0.6 copy-start.50
  68.6 1.8 copy-start
  70.3 0.7 copy-start.51
  70.6 2.5 copy-start.1
  70.6 1.6 copy-start.40
  71.4 6.8 %copy-start.34 = (bf16[8,128,640]{2,1,0:T(8,128)(2,1)}, bf16[8,128,640]{2,1,0:T(8,128)(2,1)S(1)}, u32[]{:S(2)}) copy-start(bf16[8,128,640]{2,1,0:T(8,128)(2,1)S(1)} %multiply_convert_fusion) | copy-start | bytes 3932164
  71.4 1.6 copy-start.44
  72.8 1.3 copy-start.3
  73.1 0.9 copy-start.14
  73.1 7.2 %copy-start.16 = (bf16[8,32,640]{2,1,0:T(8,128)(2,1)}, bf16[8,32,640]{2,1,0:T(8,128)(2,1)S(1)}, u32[]{:S(2)}) copy-start(bf16[8,32,640]{2,1,0:T(8,128)(2,1)S(1)} %get-tuple-element.58) | copy-start | bytes 983044
  76.3 1.1 copy-start.30
  76.3 1.1 copy-start.32
  76.3 1.1 copy-start.46
  76.4 1.2 copy-start.48
  76.6 1.0 copy-start.36
  76.6 1.1 copy-start.38
  78.8 2.8 copy-start.26
  80.3 1.3 copy-start.20
  80.3 14.5 %copy-start.19 = (bf16[128,640]{1,0:T(8,128)(2,1)S(1)}, bf16[128,640]{1,0:T(8,128)(2,1)}, u32[]{:S(2)}) copy-start(bf16[128,640]{1,0:T(8,128)(2,1)} %refs_0_.1) | copy-start | bytes 491524
  107.1 3.7 %copy-start.5 = (bf16[4,128,640]{2,1,0:T(8,128)(2,1)S(1)}, bf16[4,128,640]{2,1,0:T(8,128)(2,1)}, u32[]{:S(2)}) copy-start(bf16[4,128,640]{2,1,0:T(8,128)(2,1)} %mlp_gather.1) | copy-start | bytes 1966084
  109.9 0.8 copy-start.8
  157.9 3.4 %copy-start.9 = (bf16[8,64,640]{2,1,0:T(8,128)(2,1)S(1)}, bf16[8,64,640]{2,1,0:T(8,128)(2,1)}, u32[]{:S(2)}) copy-start(bf16[8,64,640]{2,1,0:T(8,128)(2,1)} %copy-done.8) | copy-start | bytes 1966084
  157.9 3.4 %copy-start.12 = (f32[512,512]{1,0:T(8,128)S(1)}, f32[512,512]{1,0:T(8,128)}, u32[]{:S(2)}) copy-start(f32[512,512]{1,0:T(8,128)} %copy.27) | copy-start | bytes 3145732
  157.9 3.4 %copy-start.13 = (f32[512,512]{1,0:T(8,128)S(1)}, f32[512,512]{1,0:T(8,128)}, u32[]{:S(2)}) copy-start(f32[512,512]{1,0:T(8,128)} %copy.29) | copy-start | bytes 3145732
  177.0 0.7 copy-start.17
  189.9 2.4 copy-start.27
  192.3 2.8 copy-start.28
  192.3 1.1 copy-start.37
  192.3 1.2 copy-start.39
  193.5 0.9 copy-start.47
  193.5 1.0 copy-start.49
  193.5 1.5 copy-start.41
  195.0 2.8 copy-start.4
  195.7 2.5 copy-start.31
  195.7 2.5 copy-start.33
  197.8 0.8 copy-start.10
  197.8 1.0 copy-start.11
  197.8 1.6 copy-start.6
  197.8 1.8 copy-start.54
  198.2 2.0 copy-start.53
  198.3 2.5 copy-start.22
  198.3 2.5 copy-start.24
  198.8 2.0 copy-start.43
  198.8 2.0 copy-start.52
  202.9 119.8 %all-to-all-start = ((bf16[8,192,640]{2,1,0:T(8,128)(2,1)}), bf16[8,192,640]{2,1,0:T(8,128)(2,1)}, u32[]{:S(2)}, u32[]{:S(2)}) async-start(bf16[8,192,640]{2,1,0:T(8,128)(2,1)} %pad_maximum_fusion), calls=%async_computation | async-start | bytes 3932160 | tf_op jit(solution)/shard_map/all_to_all | solution.py:330
  216.7 1.9 copy-start.23
  216.7 1.9 copy-start.25
  216.7 2.0 copy-start.42
  218.7 1.0 copy-start.15
  220.1 2.2 copy-start.2
  220.1 2.7 copy-start.7
  220.2 2.7 copy-start.21
  222.4 1.8 copy-start.29
  222.4 1.8 copy-start.35
  289.3 3.6 %copy-start.45 = (bf16[32,16,640]{2,1,0:T(8,128)(2,1)S(1)}, bf16[32,16,640]{2,1,0:T(8,128)(2,1)}, u32[]{:S(2)}) copy-start(bf16[32,16,640]{2,1,0:T(8,128)(2,1)} %get-tuple-element.24) | copy-start | bytes 1966084
  289.3 3.7 %copy-start.18 = (f32[128,640]{1,0:T(8,128)S(1)}, f32[128,640]{1,0:T(8,128)}, u32[]{:S(2)}) copy-start(f32[128,640]{1,0:T(8,128)} %copy-done.17) | copy-start | bytes 983044
  290.6 30.8 %collective-permute-start.1 = (bf16[64,640]{1,0:T(8,128)(2,1)S(1)}, bf16[64,640]{1,0:T(8,128)(2,1)S(1)}, u32[]{:S(2)}, u32[]{:S(2)}) collective-permute-start(bf16[64,640]{1,0:T(8,128)(2,1)S(1)} %reduce_sum.290), channel_id=1, source_target_pairs={{0,0},{4,1},{8,2},{12,3},{16,4},{20,5},{24,6},{28,7},{1,8},{5,9},{... | collective-permute-start | bytes 245768 | tf_op jit(solution)/shard_map/ppermute | solution.py:409
Sparse Core Ops, SparseCore 0:
  10.2 67.8 all-gather.2

commit v2 on v1

--- a/solution.py
+++ b/solution.py
@@ -167,6 +167,175 @@
     )(*arrays)
 
 
+def digit_place(digit):
+    if digit == "head_slow":
+        return lax.axis_index("head") // fast_size()
+    if digit == "head_fast":
+        return lax.rem(lax.axis_index("head"), fast_size())
+    return lax.axis_index(digit)
+
+
+def fast_size():
+    return 2 if lax.axis_size("head") % 2 == 0 else 1
+
+
+def digit_size(digit):
+    if digit == "head_slow":
+        return lax.axis_size("head") // fast_size()
+    if digit == "head_fast":
+        return fast_size()
+    return lax.axis_size(digit)
+
+
+def digit_device(digit, value):
+    if digit == "head_slow":
+        return {"head": value * fast_size() + digit_place("head_fast")}
+    if digit == "head_fast":
+        return {"head": digit_place("head_slow") * fast_size() + value}
+    return {digit: value}
+
+
+def staged_kernel(plans, greeted, *refs):
+    total = len(plans)
+    sources, targets, sems = refs[:total], refs[total : 2 * total], list(refs[2 * total :])
+    barrier = pltpu.get_barrier_semaphore()
+    waits = 0
+    for digit in greeted:
+        count, me = digit_size(digit), digit_place(digit)
+        for offset in range(1, count):
+            pl.semaphore_signal(
+                barrier,
+                inc=1,
+                device_id=digit_device(digit, lax.rem(me + offset, count)),
+                device_id_type=pl.DeviceIdType.MESH,
+            )
+            waits += 1
+    local_sems = sems[:total]
+    rest = sems[total:]
+    pairs = []
+    for plan in plans:
+        pairs.append([(rest.pop(0), rest.pop(0)) for _ in plan])
+    own = []
+    for part, plan in enumerate(plans):
+        here = tuple(digit_place(digit) for digit in reversed(plan))
+        copy = pltpu.make_async_copy(sources[part], targets[part].at[here], local_sems[part].at[0])
+        copy.start()
+        own.append(copy)
+    pl.semaphore_wait(barrier, waits)
+
+    def descriptors(part, turn, backward):
+        plan = plans[part]
+        digit = plan[turn]
+        count, me = digit_size(digit), digit_place(digit)
+        outer = tuple(digit_place(name) for name in reversed(plan[turn + 1 :]))
+        found = []
+        for offset in range(1, count):
+            to = lax.rem(me + offset, count)
+            origin = lax.rem(me + count - offset, count) if backward else me
+            source = sources[part] if turn == 0 else targets[part].at[outer + (me,)]
+            found.append(
+                pltpu.make_async_remote_copy(
+                    src_ref=source,
+                    dst_ref=targets[part].at[outer + (origin,)],
+                    send_sem=pairs[part][turn][0].at[offset],
+                    recv_sem=pairs[part][turn][1].at[origin],
+                    device_id=digit_device(digit, to),
+                    device_id_type=pl.DeviceIdType.MESH,
+                )
+            )
+        return found
+
+    most = max(len(plan) for plan in plans)
+    for turn in range(most + 1):
+        for part, plan in enumerate(plans):
+            if 0 < turn <= len(plan):
+                for copy in descriptors(part, turn - 1, True):
+                    copy.wait_recv()
+            if turn == 1:
+                own[part].wait()
+            if turn < len(plan):
+                for copy in descriptors(part, turn, False):
+                    copy.start()
+    for part, plan in enumerate(plans):
+        for turn in range(len(plan)):
+            for copy in descriptors(part, turn, False):
+                copy.wait_send()
+
+
+def staged_gather(call_id, name, parts):
+    plans = [plan for plan, _ in parts]
+    arrays = [array for _, array in parts]
+    greeted = []
+    for plan in plans:
+        greeted += [digit for digit in plan if digit not in greeted]
+    shapes = [
+        jax.ShapeDtypeStruct(
+            tuple(digit_size(digit) for digit in reversed(plan)) + array.shape, array.dtype
+        )
+        for plan, array in parts
+    ]
+    scratch = [pltpu.SemaphoreType.DMA((1,)) for _ in parts]
+    for plan in plans:
+        for digit in plan:
+            scratch += [pltpu.SemaphoreType.DMA((digit_size(digit),))] * 2
+    in_vmem = pl.BlockSpec(memory_space=pltpu.VMEM)
+    return pl.pallas_call(
+        lambda *refs: staged_kernel(plans, greeted, *refs),
+        out_shape=shapes,
+        in_specs=[in_vmem] * len(arrays),
+        out_specs=[in_vmem] * len(arrays),
+        scratch_shapes=scratch,
+        compiler_params=pltpu.CompilerParams(collective_id=call_id, has_side_effects=True),
+        name=name,
+    )(*arrays)
+
+
+def gather_rows(call_id, name, rows):
+    (blocks,) = staged_gather(call_id, name, [(("head_slow", "head_fast"), rows)])
+    return jnp.swapaxes(blocks, 0, 1).reshape(-1, rows.shape[1])
+
+
+def shifted(array, axis, offset):
+    count = lax.axis_size(axis)
+    return lax.ppermute(array, axis, [(here, (here + offset) % count) for here in range(count)])
+
+
+def gelu_parts(value):
+    root = math.sqrt(2.0 / math.pi)
+    square = value * value
+    tanh_part = jnp.tanh(root * (value + 0.044715 * value * square))
+    gelu = 0.5 * value * (1.0 + tanh_part)
+    slope = 0.5 * (1.0 + tanh_part) + 0.5 * value * (1.0 - tanh_part * tanh_part) * root * (
+        1.0 + 3.0 * 0.044715 * square
+    )
+    return gelu, slope
+
+
+def mlp_forward_kernel(rows_ref, gate_ref, up_ref, down_ref, gate_pre_ref, up_pre_ref, hidden_ref, part_ref):
+    rows = rows_ref[...]
+    gate_pre = rows_dot(rows, gate_ref[...], 1, 1)
+    up_pre = rows_dot(rows, up_ref[...], 1, 1)
+    gate_pre_ref[...] = gate_pre
+    up_pre_ref[...] = up_pre
+    hidden = (gelu_parts(gate_pre)[0] * up_pre).astype(jnp.bfloat16)
+    hidden_ref[...] = hidden
+    part_ref[...] = rows_dot(hidden, down_ref[...], 1, 0).astype(jnp.bfloat16)
+
+
+def mlp_backward_kernel(
+    rows_ref, gate_ref, up_ref, down_ref, gate_pre_ref, up_pre_ref, grad_gate_ref, grad_up_ref, part_ref
+):
+    grad_hidden = rows_dot(rows_ref[...], down_ref[...], 1, 1)
+    gelu, slope = gelu_parts(gate_pre_ref[...])
+    grad_gate = (grad_hidden * up_pre_ref[...] * slope).astype(jnp.bfloat16)
+    grad_up = (grad_hidden * gelu).astype(jnp.bfloat16)
+    grad_gate_ref[...] = grad_gate
+    grad_up_ref[...] = grad_up
+    part_ref[...] = (
+        rows_dot(grad_gate, gate_ref[...], 1, 0) + rows_dot(grad_up, up_ref[...], 1, 0)
+    ).astype(jnp.bfloat16)
+
+
 def rows_dot(left, right, left_dim, right_dim):
     return lax.dot_general(
         left, right, (((left_dim,), (right_dim,)), ((), ())), preferred_element_type=jnp.float32
@@ -205,7 +374,11 @@
     narrow = jnp.bfloat16
 
     ff_rows = jnp.concatenate([w_gate.T, w_up.T, w_down], axis=0)
-    ff_all = lax.all_gather(ff_rows, weight_axes, axis=0, tiled=False)
+    dp_count, ctx_count = lax.axis_size("dp"), lax.axis_size("ctx")
+    near_blocks = [ff_rows] + [shifted(ff_rows, "dp", offset) for offset in range(1, dp_count)]
+    ff_slots = list(near_blocks)
+    for offset in range(1, ctx_count):
+        ff_slots += [shifted(block, "ctx", offset) for block in near_blocks]
 
     to_heads = [
         (head * group_count + index, index * head_count + head)
@@ -217,17 +390,21 @@
         jnp.concatenate([w_query.T, w_out], axis=0), every_axis, to_heads
     )
     key_value_rows = jnp.concatenate([w_key.T, w_value.T], axis=0)
-    block_all, key_value_all, head_all, position_all = exchange(
+    block_all, key_value_all, head_all, position_all = staged_gather(
         1,
         "first_gather",
         [
-            ("gather", sequence_axes, block_in),
-            ("gather", every_axis, key_value_rows),
-            ("gather", weight_axes, head_rows),
-            ("gather", ("ctx",), positions.reshape(-1, 128)),
-        ],
-        every_axis,
-    )
+            (("ctx", "head_slow", "head_fast"), block_in),
+            (("dp", "ctx", "head_slow", "head_fast"), key_value_rows),
+            (("dp", "ctx"), head_rows),
+            (("ctx",), positions.reshape(-1, 128)),
+        ],
+    )
+    block_all = block_all.transpose(2, 1, 0, 3, 4)
+    key_value_all = key_value_all.transpose(3, 2, 1, 0, 4, 5).reshape(
+        every_count, 2 * key_cols, model_width
+    )
+    head_all = head_all.transpose(1, 0, 2, 3).reshape(group_count, 2 * query_cols, model_width)
     query_weight = head_all[:, :query_cols].reshape(head_width, model_width)
     out_weight = head_all[:, query_cols:].reshape(head_width, model_width)
     key_weight = key_value_all[:, :key_cols].reshape(head_width, model_width)
@@ -273,19 +450,20 @@
     branch_normed, inverse_branch = norm_rows(branch, norm_gains[1])
     middle = input_wide + branch_normed
     mlp_norm, inverse_mid = norm_rows(middle, norm_gains[2])
-    (mlp_blocks,) = exchange(
-        3, "mlp_gather", [("gather", ("head",), mlp_norm.astype(narrow))]
-    )
-    mlp_in = mlp_blocks.reshape(query_rows, model_width)
+    mlp_in = gather_rows(3, "mlp_gather", mlp_norm.astype(narrow))
 
     ff_width = group_count * ff_cols
-    gate_weight = ff_all[:, :ff_cols].reshape(ff_width, model_width)
-    up_weight = ff_all[:, ff_cols : 2 * ff_cols].reshape(ff_width, model_width)
-    down_weight = ff_all[:, 2 * ff_cols :].reshape(ff_width, model_width)
-    gate_pre = rows_dot(mlp_in, gate_weight, 1, 1)
-    up_pre = rows_dot(mlp_in, up_weight, 1, 1)
-    hidden = gelu_product(gate_pre, up_pre).astype(narrow)
-    down_part = rows_dot(hidden, down_weight, 1, 0).astype(narrow)
+    gate_weight = jnp.concatenate([block[:ff_cols] for block in ff_slots], axis=0)
+    up_weight = jnp.concatenate([block[ff_cols : 2 * ff_cols] for block in ff_slots], axis=0)
+    down_weight = jnp.concatenate([block[2 * ff_cols :] for block in ff_slots], axis=0)
+    wide_ff = jax.ShapeDtypeStruct((query_rows, ff_width), jnp.float32)
+    narrow_ff = jax.ShapeDtypeStruct((query_rows, ff_width), narrow)
+    narrow_rows = jax.ShapeDtypeStruct((query_rows, model_width), narrow)
+    gate_pre, up_pre, hidden, down_part = pl.pallas_call(
+        mlp_forward_kernel,
+        out_shape=[wide_ff, wide_ff, narrow_ff, narrow_rows],
+        name="mlp_forward",
+    )(mlp_in, gate_weight, up_weight, down_weight)
     (down_blocks,) = exchange(
         4,
         "down_scatter",
@@ -296,18 +474,12 @@
     block_out = (middle + down_normed).astype(narrow)
     cot_wide = cotangent.astype(jnp.float32)
     grad_down_raw, gain_three = norm_back(down_raw, inverse_down, norm_gains[3], cot_wide)
-    (grad_down_blocks,) = exchange(
-        5, "grad_down_gather", [("gather", ("head",), grad_down_raw.astype(narrow))]
-    )
-    grad_down_in = grad_down_blocks.reshape(query_rows, model_width)
-    grad_hidden = rows_dot(grad_down_in, down_weight, 1, 1)
-    _, gelu_pull = jax.vjp(gelu_product, gate_pre, up_pre)
-    grad_gate_raw, grad_up_raw = gelu_pull(grad_hidden)
-    grad_gate_in = grad_gate_raw.astype(narrow)
-    grad_up_in = grad_up_raw.astype(narrow)
-    grad_mlp_part = rows_dot(grad_gate_in, gate_weight, 1, 0) + rows_dot(
-        grad_up_in, up_weight, 1, 0
-    )
+    grad_down_in = gather_rows(5, "grad_down_gather", grad_down_raw.astype(narrow))
+    grad_gate_in, grad_up_in, grad_mlp_part = pl.pallas_call(
+        mlp_backward_kernel,
+        out_shape=[narrow_ff, narrow_ff, narrow_rows],
+        name="mlp_backward",
+    )(grad_down_in, gate_weight, up_weight, down_weight, gate_pre, up_pre)
     (grad_mlp_blocks,) = exchange(
         6,
         "grad_mlp_scatter",
@@ -315,28 +487,33 @@
             (
                 "scatter",
                 ("head",),
-                grad_mlp_part.astype(narrow).reshape(head_count, tok_rows, model_width),
+                grad_mlp_part.reshape(head_count, tok_rows, model_width),
             )
         ],
     )
+    slots = (ctx_count, dp_count, ff_cols, model_width)
     ff_terms = jnp.concatenate(
         [
-            rows_dot(grad_gate_in, mlp_in, 0, 0).reshape(group_count, ff_cols, model_width),
-            rows_dot(grad_up_in, mlp_in, 0, 0).reshape(group_count, ff_cols, model_width),
-            rows_dot(hidden, grad_down_in, 0, 0).reshape(group_count, ff_cols, model_width),
-        ],
-        axis=1,
-    ).astype(narrow)
-    ff_blocks = lax.all_to_all(ff_terms, weight_axes, split_axis=0, concat_axis=0, tiled=True)
+            rows_dot(grad_gate_in, mlp_in, 0, 0).astype(narrow).reshape(slots),
+            rows_dot(grad_up_in, mlp_in, 0, 0).astype(narrow).reshape(slots),
+            rows_dot(hidden, grad_down_in, 0, 0).astype(narrow).reshape(slots),
+        ],
+        axis=2,
+    )
+    ff_sums = ff_terms[0].astype(jnp.float32)
+    for offset in range(1, ctx_count):
+        ff_sums = ff_sums + shifted(ff_terms[offset], "ctx", -offset).astype(jnp.float32)
+    ff_own = ff_sums[0]
+    for offset in range(1, dp_count):
+        ff_own = ff_own + shifted(ff_sums[offset].astype(narrow), "dp", -offset).astype(
+            jnp.float32
+        )
 
     grad_mlp_in = add_up(grad_mlp_blocks)
     grad_mid_part, gain_two = norm_back(middle, inverse_mid, norm_gains[2], grad_mlp_in)
     grad_middle = cot_wide + grad_mid_part
     grad_branch_raw, gain_one = norm_back(branch, inverse_branch, norm_gains[1], grad_middle)
-    (grad_branch_blocks,) = exchange(
-        7, "grad_branch_gather", [("gather", ("head",), grad_branch_raw.astype(narrow))]
-    )
-    grad_branch = grad_branch_blocks.reshape(query_rows, model_width)
+    grad_branch = gather_rows(7, "grad_branch_gather", grad_branch_raw.astype(narrow))
     head_grad = rows_dot(grad_branch, out_weight, 1, 1).astype(narrow)
     row_delta = jnp.sum(head_grad.astype(jnp.float32) * attn_exact, axis=1, keepdims=True)
     grad_probs = rows_dot(head_grad, all_values, 1, 1)
@@ -365,13 +542,15 @@
         ],
         axis=1,
     ).astype(narrow)
+    planes = (dp_count, every_count // dp_count, key_cols, model_width)
     key_value_terms = jnp.concatenate(
         [
-            rows_dot(grad_key_in, attn_in_all, 0, 0).reshape(every_count, key_cols, model_width),
-            rows_dot(grad_value_in, attn_in_all, 0, 0).reshape(every_count, key_cols, model_width),
-        ],
-        axis=1,
-    ).astype(narrow)
+            rows_dot(grad_key_in, attn_in_all, 0, 0).reshape(planes),
+            rows_dot(grad_value_in, attn_in_all, 0, 0).reshape(planes),
+        ],
+        axis=2,
+    ).astype(narrow).transpose(1, 0, 2, 3)
+    head_terms = head_terms.reshape(dp_count, ctx_count, 2 * query_cols, model_width)
     grad_attn_blocks, head_blocks, key_value_blocks = exchange(
         8,
         "last_scatter",
@@ -381,10 +560,10 @@
                 sequence_axes,
                 grad_attn_part.astype(narrow).reshape(-1, tok_rows, model_width),
             ),
-            ("scatter", weight_axes, head_terms),
-            ("scatter", every_axis, key_value_terms),
-        ],
-        every_axis,
+            ("scatter", ("ctx",), head_terms.transpose(1, 0, 2, 3)),
+            ("scatter", sequence_axes, key_value_terms),
+        ],
+        sequence_axes,
     )
     grad_attn_in = add_up(grad_attn_blocks)
     grad_in_part, gain_zero = norm_back(input_wide, inverse_in, norm_gains[0], grad_attn_in)
@@ -403,14 +582,21 @@
         ],
         axis=0,
     )
-    (gain_blocks,) = exchange(9, "gain_gather", [("gather", every_axis, gain_terms)])
-    gains = add_up(gain_blocks)
-
+    gain_blocks, head_blocks, key_value_blocks = exchange(
+        9,
+        "depth_exchange",
+        [
+            ("gather", ("dp",), gain_terms),
+            ("scatter", ("dp",), add_up(head_blocks).astype(narrow)),
+            ("scatter", ("dp",), add_up(key_value_blocks).astype(narrow)),
+        ],
+    )
     head_own = lax.ppermute(add_up(head_blocks).astype(narrow), every_axis, to_owners).astype(
         jnp.float32
     )
+    (gain_blocks,) = exchange(10, "gain_gather", [("gather", sequence_axes, add_up(gain_blocks))])
+    gains = add_up(gain_blocks)
     key_value_own = add_up(key_value_blocks)
-    ff_own = add_up(ff_blocks)
     return (
         block_out,
         d_block_in,

time: 337 us -> 316 us (0.938)
  Pallas kernels: 209 us -> 180 us
  matrix products: 32.2 us -> 14.5 us
  between operations: 15 us -> 1.51 us
  waiting for transfers between devices: 0.04 us -> 11.5 us
  local copies, waits for them, and re-layouts: 24.4 us -> 34.9 us
  starting transfers between devices: 15.2 us -> 25.4 us
  other arithmetic: 36 us -> 42.9 us
    pallas_call x9 -> x6, Pallas kernels: 209 us -> 103 us  [exchange(): pl.pallas_call(lambda *refs: exchange_kernel(kinds, greet, counts, *refs)...]
    pallas_call x0 -> x6, Pallas kernels: none -> 76.8 us  [the longest x4 67.4 us: staged_gather(): pl.pallas_call(lambda *refs: staged_kernel(plans, greeted, *refs), out_sh...]
    ppermute x0 -> x11, starting transfers between devices: none -> 24.1 us  [shifted(): lax.ppermute(array, axis, [(here, (here + offset) % count) for here in ra...]
    dot_general x27 -> x21, matrix products: 32.2 us -> 14.5 us  [rows_dot(): lax.dot_general(left, right, (((left_dim,), (right_dim,)), ((), ())), pre...]
    all_to_all x1 -> x0, starting transfers between devices: 13.8 us -> none  [local(): lax.all_to_all(ff_terms, weight_axes, split_axis=0, concat_axis=0, tiled=...]
    unnamed x110 -> x96, local copies, waits for them, and re-layouts: 7.62 us -> 21.3 us
    ppermute x0 -> x11, waiting for transfers between devices: none -> 11.5 us  [shifted(): lax.ppermute(array, axis, [(here, (here + offset) % count) for here in ra...]
    dot_general x3 -> x0, local copies, waits for them, and re-layouts: 7.65 us -> none  [rows_dot(): lax.dot_general(left, right, (((left_dim,), (right_dim,)), ((), ())), pre...]
  transfers between devices with their start and end apart: 4 -> 13, of which waited for: 0 -> 3; matrix products, arithmetic and copies ran while one was open for 10% -> 17% of each run, Pallas kernels for 49% -> 42%
where the time goes in v2:
time: 316 us; the launch traced here: 311 us
  Pallas kernels  180 us (57%)
  other arithmetic  42.9 us (14%)
  local copies, waits for them, and re-layouts  34.9 us (11%)
  starting transfers between devices  25.4 us (8%)
  matrix products  14.5 us (5%)
  waiting for transfers between devices  11.5 us (4%)
    pallas_call x6, Pallas kernels, exchange(): pl.pallas_call(lambda *refs: exchange_kernel(kinds, greet, counts, *refs)...  103 us
    pallas_call x4, Pallas kernels, staged_gather(): pl.pallas_call(lambda *refs: staged_kernel(plans, greeted, *refs), out_sh...  67.4 us
    ppermute x11, starting transfers between devices, shifted(): lax.ppermute(array, axis, [(here, (here + offset) % count) for here in ra...  24.1 us
    unnamed x96, local copies, waits for them, and re-layouts  21.3 us
    dot_general x21, matrix products, rows_dot(): lax.dot_general(left, right, (((left_dim,), (right_dim,)), ((), ())), pre...  14.5 us
    reduce_sum x10, other arithmetic, add_up(): return jnp.sum(blocks.astype(jnp.float32), axis=0)  12.5 us
    ppermute x11, waiting for transfers between devices, shifted(): lax.ppermute(array, axis, [(here, (here + offset) % count) for here in ra...  11.5 us
  transfers between devices with their start and end apart: 13, of which 3 were waited for; matrix products, arithmetic and copies ran while one was open for 17% of the time, Pallas kernels for 42%

profile of v2, /device:TPU:0, one launch (start us, length us, event | category | flops | bytes accessed | tf_op | source)
XLA Modules:
  0.0 310.7 jit_solution(18232108611710130745)
XLA Ops:
  0.6 1.7 pad_maximum_fusion.6
  2.3 3.1 collective-permute-start.1
  5.4 2.6 collective-permute-start.2
  8.0 1.3 collective-permute-start.3
  9.3 1.5 collective-permute-start.4
  12.3 1.5 constant_dynamic-update-slice_fusion.2
  13.8 1.6 constant_dynamic-update-slice_fusion
  15.4 0.9 slice_reduce_fusion
  17.8 1.3 pad_maximum_fusion.8.refs_1_
  19.7 37.1 %first_gather.1 = (bf16[2,2,2,128,640]{4,3,2,1,0:T(8,128)(2,1)}, bf16[2,2,2,4,16,640]{5,4,3,2,1,0:T(8,128)(2,1)}, bf16[2,4,64,640]{3,2,1,0:T(8,128)(2,1)}, s32[2,4,128]{2,1,0:T(4,128)}) custom-call(bf16[128,640]{1,0:T(8,128)(2,1)} %refs_0_.1, bf16[16,640]{1,0:T(8,128)(2,1)} %pad_maximum_fusion.8.refs_1_, bf16[64,640]{1,0:T(8,128)(2,1)} %copy-done.38, ...), custom_call_target="tpu_custom_call" | custom-call | tf_op jit(solution)/shard_map/first_gather/pallas_call | solution.py:282
  56.8 1.7 multiply_reduce_fusion
  59.1 1.1 copy-done.32
  64.7 2.1 multiply_cosine_fusion
  69.1 1.4 fusion.66
  70.5 1.3 convolution_convert_fusion
  71.8 10.8 %branch_scatter.1 = bf16[4,128,640]{2,1,0:T(8,128)(2,1)} custom-call(bf16[4,128,640]{2,1,0:T(8,128)(2,1)} %bitcast.151), custom_call_target="tpu_custom_call" | custom-call | tf_op jit(solution)/shard_map/branch_scatter/pallas_call | solution.py:159
  82.6 1.2 convert_reduce_fusion.3
  84.4 1.1 multiply_reduce_fusion.13
  87.1 10.3 %mlp_gather.1 = bf16[2,2,128,640]{3,2,1,0:T(8,128)(2,1)} custom-call(bf16[128,640]{1,0:T(8,128)(2,1)} %multiply_convert_fusion.2.refs_0_), custom_call_target="tpu_custom_call" | custom-call | tf_op jit(solution)/shard_map/mlp_gather/pallas_call | solution.py:282
  97.3 2.0 copy.45
  99.3 3.0 collective-permute-start.5
  102.4 1.9 collective-permute-start.7
  104.4 1.7 slice_dynamic-update-slice_fusion.6
  106.1 1.7 slice_dynamic-update-slice_fusion.5
  107.7 1.7 slice_dynamic-update-slice_fusion.4
  109.4 1.7 slice_dynamic-update-slice_fusion.3
  111.8 2.8 collective-permute-done.6
  115.3 4.0 %collective-permute-done.7 = bf16[192,640]{1,0:T(8,128)(2,1)S(1)} collective-permute-done((bf16[192,640]{1,0:T(8,128)(2,1)}, bf16[192,640]{1,0:T(8,128)(2,1)S(1)}, u32[]{:S(2)}, u32[]{:S(2)}) %collective-permute-start.7) | collective-permute-done | bytes 245792 | tf_op jit(solution)/shard_map/ppermute | solution.py:300
  120.1 4.2 %mlp_forward.1 = (f32[512,512]{1,0:T(8,128)}, f32[512,512]{1,0:T(8,128)}, bf16[512,512]{1,0:T(8,128)(2,1)}, bf16[512,640]{1,0:T(8,128)(2,1)}) custom-call(bf16[512,640]{1,0:T(8,128)(2,1)} %bitcast.142, bf16[512,640]{1,0:T(8,128)(2,1)} %get-tuple-element.86.gate_ref, bf16[512,640]{1,0:T(8,128)(2,1)} %get-tuple-element.85.up_ref, ...), custom_call_target="tpu_custom_call" | custom-call | tf_op jit(solution)/shard_map/mlp_forward/pallas_call | solution.py:462
  124.3 11.1 %down_scatter.1 = bf16[4,128,640]{2,1,0:T(8,128)(2,1)} custom-call(bf16[4,128,640]{2,1,0:T(8,128)(2,1)} %bitcast.163), custom_call_target="tpu_custom_call" | custom-call | tf_op jit(solution)/shard_map/down_scatter/pallas_call | solution.py:159
  135.5 1.3 convert_reduce_fusion.2
  136.8 1.1 fusion.33
  137.9 1.8 fusion.30
  139.7 9.9 %grad_down_gather.1 = bf16[2,2,128,640]{3,2,1,0:T(8,128)(2,1)} custom-call(bf16[128,640]{1,0:T(8,128)(2,1)} %get-tuple-element.82.refs_0_), custom_call_target="tpu_custom_call" | custom-call | tf_op jit(solution)/shard_map/grad_down_gather/pallas_call | solution.py:282
  149.7 2.0 copy.46
  151.6 5.2 %mlp_backward.1 = (bf16[512,512]{1,0:T(8,128)(2,1)}, bf16[512,512]{1,0:T(8,128)(2,1)}, bf16[512,640]{1,0:T(8,128)(2,1)}) custom-call(bf16[512,640]{1,0:T(8,128)(2,1)} %bitcast.145, bf16[512,640]{1,0:T(8,128)(2,1)} %get-tuple-element.86.gate_ref, bf16[512,640]{1,0:T(8,128)(2,1)} %get-tuple-element.85.up_ref, bf16[512,640]{1,0:T(8,128)(2,1)} %get-tuple-element.84.down_ref, ...), custom_call_target="tpu_custom_call" | custom-call | tf_op jit(solution)/shard_map/mlp_backward/pallas_call | solution.py:478
  156.9 10.1 %grad_mlp_scatter.1 = bf16[4,128,640]{2,1,0:T(8,128)(2,1)} custom-call(bf16[4,128,640]{2,1,0:T(8,128)(2,1)} %bitcast.162), custom_call_target="tpu_custom_call" | custom-call | tf_op jit(solution)/shard_map/grad_mlp_scatter/pallas_call | solution.py:159
  167.0 1.2 convert_reduce_fusion.1
  168.2 1.1 multiply_reduce_fusion.8
  169.4 1.3 multiply_reduce_fusion.9
  172.2 10.1 %grad_branch_gather.1 = bf16[2,2,128,640]{3,2,1,0:T(8,128)(2,1)} custom-call(bf16[128,640]{1,0:T(8,128)(2,1)} %subtract_convert_fusion.2.refs_0_), custom_call_target="tpu_custom_call" | custom-call | tf_op jit(solution)/shard_map/grad_branch_gather/pallas_call | solution.py:282
  182.3 1.1 copy.47
  183.5 1.6 multiply_reduce_fusion.6
  188.2 2.1 fusion.15
  193.1 1.3 copy-done.2
  196.3 1.2 convert_element_type.202
  202.0 1.0 slice_bitcast_fusion
  203.1 1.7 collective-permute-start.9
  205.2 0.9 maximum_bitcast_fusion.refs_1_
  206.1 0.9 maximum_bitcast_fusion.1.refs_2_
  207.0 49.4 %last_scatter.1 = (bf16[8,128,640]{2,1,0:T(8,128)(2,1)}, bf16[2,4,64,640]{3,2,1,0:T(8,128)(2,1)}, bf16[8,4,16,640]{3,2,1,0:T(8,128)(2,1)}) custom-call(bf16[8,128,640]{2,1,0:T(8,128)(2,1)} %bitcast.133, bf16[2,4,64,640]{3,2,1,0:T(8,128)(2,1)} %maximum_bitcast_fusion.refs_1_, bf16[8,4,16,640]{3,2,1,0:T(8,128)(2,1)} %maximum_bitcast_fusion.1.refs_2_), custom_call_target="tpu_custom_call" | custom-call | tf_op jit(solution)/shard_map/last_scatter/pallas_call | solution.py:159
  256.4 1.5 convert_reduce_fusion
  258.1 2.0 reduce_sum.313.refs_1_
  260.1 1.8 reduce_sum.314.refs_2_
  262.6 15.2 %depth_exchange.1 = (f32[4,8,640]{2,1,0:T(8,128)}, bf16[4,64,640]{2,1,0:T(8,128)(2,1)}, bf16[4,16,640]{2,1,0:T(8,128)(2,1)}) custom-call(f32[8,640]{1,0:T(8,128)} %concatenate.61.refs_0_, bf16[4,64,640]{2,1,0:T(8,128)(2,1)} %reduce_sum.313.refs_1_, bf16[4,16,640]{2,1,0:T(8,128)(2,1)} %reduce_sum.314.refs_2_), custom_call_target="tpu_custom_call" | custom-call | tf_op jit(solution)/shard_map/depth_exchange/pallas_call | solution.py:159
  277.9 1.0 reduce_sum.317
  279.6 0.9 convert_reduce_fusion.4
  281.3 2.7 fusion.61
  284.1 5.4 %collective-permute-start.12 = (bf16[192,640]{1,0:T(8,128)(2,1)S(1)}, bf16[192,640]{1,0:T(8,128)(2,1)S(1)}, u32[]{:S(2)}, u32[]{:S(2)}) collective-permute-start(bf16[192,640]{1,0:T(8,128)(2,1)S(1)} %get-tuple-element.75), channel_id=1, source_target_pairs={{0,8},{8,16},{16,24},{24,0},{1,9},{9,17},{17,25},{25,1},{2,10},{10... | collective-permute-start | bytes 737288 | tf_op jit(solution)/shard_map/ppermute | solution.py:300
  289.6 3.4 %collective-permute-start.11 = (bf16[192,640]{1,0:T(8,128)(2,1)S(1)}, bf16[192,640]{1,0:T(8,128)(2,1)S(1)}, u32[]{:S(2)}, u32[]{:S(2)}) collective-permute-start(bf16[192,640]{1,0:T(8,128)(2,1)S(1)} %get-tuple-element.76), channel_id=1, source_target_pairs={{0,16},{8,24},{16,0},{24,8},{1,17},{9,25},{17,1},{25,9},{2,18},{10... | collective-permute-start | bytes 737288 | tf_op jit(solution)/shard_map/ppermute | solution.py:300
  294.2 6.5 %gain_gather.1 = f32[8,8,640]{2,1,0:T(8,128)} custom-call(f32[8,640]{1,0:T(8,128)} %reduce_sum.315.refs_0_), custom_call_target="tpu_custom_call" | custom-call | tf_op jit(solution)/shard_map/gain_gather/pallas_call | solution.py:159
  300.7 0.9 reduce_sum.316
  304.1 4.7 %collective-permute-done.11 = bf16[192,640]{1,0:T(8,128)(2,1)S(1)} collective-permute-done((bf16[192,640]{1,0:T(8,128)(2,1)S(1)}, bf16[192,640]{1,0:T(8,128)(2,1)S(1)}, u32[]{:S(2)}, u32[]{:S(2)}) %collective-permute-start.11) | collective-permute-done | bytes 245792 | tf_op jit(solution)/shard_map/ppermute | solution.py:300
  308.8 1.1 fusion.26
  (182 shorter events, 36.0 us)
Async XLA Ops:
  2.3 97.0 %collective-permute-start.1 = (bf16[192,640]{1,0:T(8,128)(2,1)}, bf16[192,640]{1,0:T(8,128)(2,1)}, u32[]{:S(2)}, u32[]{:S(2)}) collective-permute-start(bf16[192,640]{1,0:T(8,128)(2,1)} %pad_maximum_fusion.6), channel_id=1, source_target_pairs={{0,8},{8,16},{16,24},{24,0},{1,9},{9,17},{17,25},{25,1},{2,10},{10... | collective-permute-start | bytes 737288 | tf_op jit(solution)/shard_map/ppermute | solution.py:300
  5.4 97.0 %collective-permute-start.2 = (bf16[192,640]{1,0:T(8,128)(2,1)}, bf16[192,640]{1,0:T(8,128)(2,1)}, u32[]{:S(2)}, u32[]{:S(2)}) collective-permute-start(bf16[192,640]{1,0:T(8,128)(2,1)} %pad_maximum_fusion.6), channel_id=1, source_target_pairs={{0,16},{8,24},{16,0},{24,8},{1,17},{9,25},{17,1},{25,9},{2,18},{10... | collective-permute-start | bytes 737288 | tf_op jit(solution)/shard_map/ppermute | solution.py:300
  8.0 94.5 %collective-permute-start.3 = (bf16[192,640]{1,0:T(8,128)(2,1)}, bf16[192,640]{1,0:T(8,128)(2,1)}, u32[]{:S(2)}, u32[]{:S(2)}) collective-permute-start(bf16[192,640]{1,0:T(8,128)(2,1)} %pad_maximum_fusion.6), channel_id=1, source_target_pairs={{0,24},{8,0},{16,8},{24,16},{1,25},{9,1},{17,9},{25,17},{2,26},{10... | collective-permute-start | bytes 737288 | tf_op jit(solution)/shard_map/ppermute | solution.py:300
  9.3 100.1 %collective-permute-start.4 = (bf16[192,640]{1,0:T(8,128)(2,1)}, bf16[192,640]{1,0:T(8,128)(2,1)}, u32[]{:S(2)}, u32[]{:S(2)}) collective-permute-start(bf16[192,640]{1,0:T(8,128)(2,1)} %pad_maximum_fusion.6), channel_id=1, source_target_pairs={{0,4},{4,0},{1,5},{5,1},{2,6},{6,2},{3,7},{7,3},{8,12},{12,8},{9,1... | collective-permute-start | bytes 737288 | tf_op jit(solution)/shard_map/ppermute | solution.py:300
  11.6 7.5 %collective-permute-start = (bf16[64,640]{1,0:T(8,128)(2,1)S(1)}, bf16[64,640]{1,0:T(8,128)(2,1)S(1)}, u32[]{:S(2)}, u32[]{:S(2)}) collective-permute-start(bf16[64,640]{1,0:T(8,128)(2,1)S(1)} %pad_maximum_fusion.7), channel_id=1, source_target_pairs={{0,0},{1,4},{2,8},{3,12},{4,16},{5,20},{6,24},{7,28},{8,1},{9,5},{... | collective-permute-start | bytes 245768 | tf_op jit(solution)/shard_map/ppermute | solution.py:389
  19.1 0.6 copy-start.38
  56.8 1.8 copy-start
  59.0 1.2 copy-start.32
  59.1 2.6 copy-start.25
  60.2 0.9 copy-start.12
  61.1 8.0 %copy-start.19 = (bf16[1024,256]{1,0:T(8,128)(2,1)}, bf16[1024,256]{1,0:T(8,128)(2,1)S(1)}, u32[]{:S(2)}) copy-start(bf16[1024,256]{1,0:T(8,128)(2,1)S(1)} %convolution_convert_fusion.5) | copy-start | bytes 1572868
  61.7 0.7 copy-start.39
  61.7 1.1 copy-start.31
  63.0 0.7 copy-start.7
  63.0 7.6 %copy-start.9 = (bf16[8,32,640]{2,1,0:T(8,128)(2,1)}, bf16[8,32,640]{2,1,0:T(8,128)(2,1)S(1)}, u32[]{:S(2)}) copy-start(bf16[8,32,640]{2,1,0:T(8,128)(2,1)S(1)} %get-tuple-element.77) | copy-start | bytes 983044
  63.2 1.5 copy-start.1
  64.2 2.6 copy-start.3
  66.8 0.8 copy-start.21
  66.8 1.0 copy-start.23
  66.8 1.7 copy-start.33
  66.8 1.7 copy-start.35
  67.1 1.5 copy-start.27
  67.1 1.5 copy-start.29
  70.5 1.3 copy-start.17
  85.6 0.7 copy-start.5
  99.3 11.8 %collective-permute-start.5 = (bf16[192,640]{1,0:T(8,128)(2,1)}, bf16[192,640]{1,0:T(8,128)(2,1)S(1)}, u32[]{:S(2)}, u32[]{:S(2)}) collective-permute-start(bf16[192,640]{1,0:T(8,128)(2,1)} %collective-permute-done.1), channel_id=1, source_target_pairs={{0,4},{4,0},{1,5},{5,1},{2,6},{6,2},{3,7},{7,3},{8,12},{12,8},{9,1... | collective-permute-start | bytes 737288 | tf_op jit(solution)/shard_map/ppermute | solution.py:300
  102.4 12.3 %collective-permute-start.6 = (bf16[192,640]{1,0:T(8,128)(2,1)}, bf16[192,640]{1,0:T(8,128)(2,1)S(1)}, u32[]{:S(2)}, u32[]{:S(2)}) collective-permute-start(bf16[192,640]{1,0:T(8,128)(2,1)} %collective-permute-done.2), channel_id=1, source_target_pairs={{0,4},{4,0},{1,5},{5,1},{2,6},{6,2},{3,7},{7,3},{8,12},{12,8},{9,1... | collective-permute-start | bytes 737288 | tf_op jit(solution)/shard_map/ppermute | solution.py:300
  102.4 16.9 %collective-permute-start.7 = (bf16[192,640]{1,0:T(8,128)(2,1)}, bf16[192,640]{1,0:T(8,128)(2,1)S(1)}, u32[]{:S(2)}, u32[]{:S(2)}) collective-permute-start(bf16[192,640]{1,0:T(8,128)(2,1)} %collective-permute-done.3), channel_id=1, source_target_pairs={{0,4},{4,0},{1,5},{5,1},{2,6},{6,2},{3,7},{7,3},{8,12},{12,8},{9,1... | collective-permute-start | bytes 737288 | tf_op jit(solution)/shard_map/ppermute | solution.py:300
  135.4 2.5 copy-start.6
  167.0 4.4 %copy-start.40 = (f32[128]{0:T(128)S(1)}, f32[128]{0:T(128)}, u32[]{:S(2)}) copy-start(f32[128]{0:T(128)} %get-tuple-element.120) | copy-start | bytes 1540
  170.7 0.7 copy-start.10
  183.5 2.2 copy-start.20
  185.7 1.0 copy-start.28
  185.7 1.0 copy-start.30
  186.7 0.9 copy-start.34
  186.7 1.0 copy-start.36
  190.4 1.1 copy-start.13
  191.5 1.0 copy-start.22
  191.5 1.2 copy-start.24
  191.5 1.4 copy-start.4
  192.7 1.8 copy-start.2
  194.9 1.0 copy-start.8
  196.3 1.8 copy-start.26
  198.7 1.1 copy-start.15
  198.7 1.2 copy-start.41
  199.3 1.2 copy-start.14
  199.3 1.3 copy-start.43
  199.9 1.3 copy-start.42
  202.0 2.8 copy-start.18
  203.1 78.3 %collective-permute-start.9 = (bf16[4,192,640]{2,1,0:T(8,128)(2,1)}, bf16[4,192,640]{2,1,0:T(8,128)(2,1)}, u32[]{:S(2)}, u32[]{:S(2)}) collective-permute-start(bf16[4,192,640]{2,1,0:T(8,128)(2,1)} %slice_bitcast_fusion), channel_id=1, source_target_pairs={{0,4},{4,0},{1,5},{5,1},{2,6},{6,2},{3,7},{7,3},{8,12},{12,8},{9,1... | collective-permute-start | bytes 2949128 | tf_op jit(solution)/shard_map/ppermute | solution.py:300
  207.0 50.9 %copy-start.16 = (bf16[128,640]{1,0:T(8,128)(2,1)S(1)}, bf16[128,640]{1,0:T(8,128)(2,1)}, u32[]{:S(2)}) copy-start(bf16[128,640]{1,0:T(8,128)(2,1)} %refs_0_.1) | copy-start | bytes 491524
  257.9 22.6 %copy-start.11 = (f32[128,640]{1,0:T(8,128)S(1)}, f32[128,640]{1,0:T(8,128)}, u32[]{:S(2)}) copy-start(f32[128,640]{1,0:T(8,128)} %copy-done.10) | copy-start | bytes 983044
  278.9 23.9 %collective-permute-start.8 = (bf16[64,640]{1,0:T(8,128)(2,1)S(1)}, bf16[64,640]{1,0:T(8,128)(2,1)S(1)}, u32[]{:S(2)}, u32[]{:S(2)}) collective-permute-start(bf16[64,640]{1,0:T(8,128)(2,1)S(1)} %reduce_sum.317), channel_id=1, source_target_pairs={{0,0},{4,1},{8,2},{12,3},{16,4},{20,5},{24,6},{28,7},{1,8},{5,9},{... | collective-permute-start | bytes 245768 | tf_op jit(solution)/shard_map/ppermute | solution.py:594
  281.3 12.3 %copy-start.37 = (f32[4,8,640]{2,1,0:T(8,128)S(1)}, f32[4,8,640]{2,1,0:T(8,128)}, u32[]{:S(2)}) copy-start(f32[4,8,640]{2,1,0:T(8,128)} %get-tuple-element.39) | copy-start | bytes 245764
  284.1 20.0 %collective-permute-start.12 = (bf16[192,640]{1,0:T(8,128)(2,1)S(1)}, bf16[192,640]{1,0:T(8,128)(2,1)S(1)}, u32[]{:S(2)}, u32[]{:S(2)}) collective-permute-start(bf16[192,640]{1,0:T(8,128)(2,1)S(1)} %get-tuple-element.75), channel_id=1, source_target_pairs={{0,8},{8,16},{16,24},{24,0},{1,9},{9,17},{17,25},{25,1},{2,10},{10... | collective-permute-start | bytes 737288 | tf_op jit(solution)/shard_map/ppermute | solution.py:300
  289.6 19.2 %collective-permute-start.11 = (bf16[192,640]{1,0:T(8,128)(2,1)S(1)}, bf16[192,640]{1,0:T(8,128)(2,1)S(1)}, u32[]{:S(2)}, u32[]{:S(2)}) collective-permute-start(bf16[192,640]{1,0:T(8,128)(2,1)S(1)} %get-tuple-element.76), channel_id=1, source_target_pairs={{0,16},{8,24},{16,0},{24,8},{1,17},{9,25},{17,1},{25,9},{2,18},{10... | collective-permute-start | bytes 737288 | tf_op jit(solution)/shard_map/ppermute | solution.py:300
  293.0 15.8 %collective-permute-start.10 = (bf16[192,640]{1,0:T(8,128)(2,1)S(1)}, bf16[192,640]{1,0:T(8,128)(2,1)S(1)}, u32[]{:S(2)}, u32[]{:S(2)}) collective-permute-start(bf16[192,640]{1,0:T(8,128)(2,1)S(1)} %get-tuple-element.74), channel_id=1, source_target_pairs={{0,24},{8,0},{16,8},{24,16},{1,25},{9,1},{17,9},{25,17},{2,26},{10... | collective-permute-start | bytes 737288 | tf_op jit(solution)/shard_map/ppermute | solution.py:300

commit v3 on v2

--- a/solution.py
+++ b/solution.py
@@ -103,7 +103,8 @@
     locals_started = []
     for part, (kind, axes) in enumerate(kinds):
         me = place_in(axes)
-        source = sources[part].at[me] if kind == "scatter" else sources[part]
+        source = {"scatter": me, "relative": 0}.get(kind)
+        source = sources[part] if source is None else sources[part].at[source]
         copy = pltpu.make_async_copy(source, targets[part].at[me], sems[3 * part + 2].at[0])
         copy.start()
         locals_started.append(copy)
@@ -115,7 +116,8 @@
         me = place_in(axes)
         to = lax.rem(me + offset, count)
         origin = lax.rem(me + count - offset, count) if backward else me
-        source = sources[part].at[to] if kind == "scatter" else sources[part]
+        source = {"scatter": to, "relative": lax.rem(count - offset, count)}.get(kind)
+        source = sources[part] if source is None else sources[part].at[source]
         return pltpu.make_async_remote_copy(
             src_ref=source,
             dst_ref=targets[part].at[origin],
@@ -140,11 +142,11 @@
     arrays = [array for _, _, array in parts]
     counts = tuple(lax.axis_size(axes) for _, axes in kinds)
     if greet_axes is None:
-        greet_axes = kinds[0][1]
-    greet = ((greet_axes, lax.axis_size(greet_axes)),)
+        greet_axes = (kinds[0][1],)
+    greet = tuple((axes, lax.axis_size(axes)) for axes in greet_axes)
     shapes = [
         jax.ShapeDtypeStruct(
-            array.shape if kind == "scatter" else (count,) + array.shape, array.dtype
+            (count,) + array.shape if kind == "gather" else array.shape, array.dtype
         )
         for (kind, _, array), count in zip(parts, counts)
     ]
@@ -291,8 +293,8 @@
 
 
 def gather_rows(call_id, name, rows):
-    (blocks,) = staged_gather(call_id, name, [(("head_slow", "head_fast"), rows)])
-    return jnp.swapaxes(blocks, 0, 1).reshape(-1, rows.shape[1])
+    (blocks,) = exchange(call_id, name, [("gather", ("head",), rows)])
+    return blocks.reshape(-1, rows.shape[1])
 
 
 def shifted(array, axis, offset):
@@ -375,10 +377,6 @@
 
     ff_rows = jnp.concatenate([w_gate.T, w_up.T, w_down], axis=0)
     dp_count, ctx_count = lax.axis_size("dp"), lax.axis_size("ctx")
-    near_blocks = [ff_rows] + [shifted(ff_rows, "dp", offset) for offset in range(1, dp_count)]
-    ff_slots = list(near_blocks)
-    for offset in range(1, ctx_count):
-        ff_slots += [shifted(block, "ctx", offset) for block in near_blocks]
 
     to_heads = [
         (head * group_count + index, index * head_count + head)
@@ -400,6 +398,9 @@
             (("ctx",), positions.reshape(-1, 128)),
         ],
     )
+    block_all, ff_rows = lax.optimization_barrier((block_all, ff_rows))
+    near_blocks = [ff_rows] + [shifted(ff_rows, "dp", offset) for offset in range(1, dp_count)]
+    ff_across = [shifted(ff_rows, "ctx", offset) for offset in range(1, ctx_count)]
     block_all = block_all.transpose(2, 1, 0, 3, 4)
     key_value_all = key_value_all.transpose(3, 2, 1, 0, 4, 5).reshape(
         every_count, 2 * key_cols, model_width
@@ -450,6 +451,11 @@
     branch_normed, inverse_branch = norm_rows(branch, norm_gains[1])
     middle = input_wide + branch_normed
     mlp_norm, inverse_mid = norm_rows(middle, norm_gains[2])
+    mlp_norm, near_blocks, ff_across = lax.optimization_barrier((mlp_norm, near_blocks, ff_across))
+    ff_slots = list(near_blocks)
+    for offset in range(1, ctx_count):
+        ff_slots += [ff_across[offset - 1]]
+        ff_slots += [shifted(block, "ctx", offset) for block in near_blocks[1:]]
     mlp_in = gather_rows(3, "mlp_gather", mlp_norm.astype(narrow))
 
     ff_width = group_count * ff_cols
@@ -480,7 +486,17 @@
         out_shape=[narrow_ff, narrow_ff, narrow_rows],
         name="mlp_backward",
     )(grad_down_in, gate_weight, up_weight, down_weight, gate_pre, up_pre)
-    (grad_mlp_blocks,) = exchange(
+    slots = (ctx_count, dp_count, ff_cols, model_width)
+    ff_terms = jnp.concatenate(
+        [
+            rows_dot(grad_gate_in, mlp_in, 0, 0).astype(narrow).reshape(slots),
+            rows_dot(grad_up_in, mlp_in, 0, 0).astype(narrow).reshape(slots),
+            rows_dot(hidden, grad_down_in, 0, 0).astype(narrow).reshape(slots),
+        ],
+        axis=2,
+    )
+    half = dp_count // 2
+    grad_mlp_blocks, ff_early = exchange(
         6,
         "grad_mlp_scatter",
         [
@@ -488,32 +504,26 @@
                 "scatter",
                 ("head",),
                 grad_mlp_part.reshape(head_count, tok_rows, model_width),
-            )
-        ],
-    )
-    slots = (ctx_count, dp_count, ff_cols, model_width)
-    ff_terms = jnp.concatenate(
-        [
-            rows_dot(grad_gate_in, mlp_in, 0, 0).astype(narrow).reshape(slots),
-            rows_dot(grad_up_in, mlp_in, 0, 0).astype(narrow).reshape(slots),
-            rows_dot(hidden, grad_down_in, 0, 0).astype(narrow).reshape(slots),
-        ],
-        axis=2,
-    )
-    ff_sums = ff_terms[0].astype(jnp.float32)
-    for offset in range(1, ctx_count):
-        ff_sums = ff_sums + shifted(ff_terms[offset], "ctx", -offset).astype(jnp.float32)
-    ff_own = ff_sums[0]
-    for offset in range(1, dp_count):
-        ff_own = ff_own + shifted(ff_sums[offset].astype(narrow), "dp", -offset).astype(
-            jnp.float32
-        )
-
+            ),
+            ("relative", ("ctx",), ff_terms[:, :half]),
+        ],
+        (("head",), ("ctx",)),
+    )
     grad_mlp_in = add_up(grad_mlp_blocks)
     grad_mid_part, gain_two = norm_back(middle, inverse_mid, norm_gains[2], grad_mlp_in)
     grad_middle = cot_wide + grad_mid_part
     grad_branch_raw, gain_one = norm_back(branch, inverse_branch, norm_gains[1], grad_middle)
-    grad_branch = gather_rows(7, "grad_branch_gather", grad_branch_raw.astype(narrow))
+    grad_branch_blocks, ff_late = exchange(
+        7,
+        "grad_branch_gather",
+        [
+            ("gather", ("head",), grad_branch_raw.astype(narrow)),
+            ("relative", ("ctx",), ff_terms[:, half:]),
+        ],
+        (("head",), ("ctx",)),
+    )
+    grad_branch = grad_branch_blocks.reshape(query_rows, model_width)
+    ff_sums = jnp.concatenate([add_up(ff_early), add_up(ff_late)], axis=0).astype(narrow)
     head_grad = rows_dot(grad_branch, out_weight, 1, 1).astype(narrow)
     row_delta = jnp.sum(head_grad.astype(jnp.float32) * attn_exact, axis=1, keepdims=True)
     grad_probs = rows_dot(head_grad, all_values, 1, 1)
@@ -551,7 +561,7 @@
         axis=2,
     ).astype(narrow).transpose(1, 0, 2, 3)
     head_terms = head_terms.reshape(dp_count, ctx_count, 2 * query_cols, model_width)
-    grad_attn_blocks, head_blocks, key_value_blocks = exchange(
+    grad_attn_blocks, head_blocks, key_value_blocks, ff_blocks = exchange(
         8,
         "last_scatter",
         [
@@ -562,9 +572,11 @@
             ),
             ("scatter", ("ctx",), head_terms.transpose(1, 0, 2, 3)),
             ("scatter", sequence_axes, key_value_terms),
-        ],
-        sequence_axes,
-    )
+            ("relative", ("dp",), ff_sums),
+        ],
+        (sequence_axes, ("dp",)),
+    )
+    ff_own = add_up(ff_blocks)
     grad_attn_in = add_up(grad_attn_blocks)
     grad_in_part, gain_zero = norm_back(input_wide, inverse_in, norm_gains[0], grad_attn_in)
     d_block_in = (grad_middle + grad_in_part).astype(narrow)

time: 316 us -> 282 us (0.89); the launches traced: 311 us -> 280 us
  starting transfers between devices: 25.4 us -> 10.6 us
  waiting for transfers between devices: 11.5 us -> 0.02 us
  local copies, waits for them, and re-layouts: 34.9 us -> 28.3 us
  matrix products: 14.5 us -> 20.8 us
    pallas_call x4 -> x1, Pallas kernels: 67.4 us -> 31.6 us  [staged_gather(): pl.pallas_call(lambda *refs: staged_kernel(plans, greeted, *refs), out_sh...]
    pallas_call x6 -> x9, Pallas kernels: 103 us -> 136 us  [exchange(): pl.pallas_call(lambda *refs: exchange_kernel(kinds, greet, counts, *refs)...]
    ppermute x11 -> x7, starting transfers between devices: 24.1 us -> 9.28 us  [shifted(): lax.ppermute(array, axis, [(here, (here + offset) % count) for here in ra...]
    ppermute x11 -> x7, waiting for transfers between devices: 11.5 us -> 0.02 us  [shifted(): lax.ppermute(array, axis, [(here, (here + offset) % count) for here in ra...]
    dot_general x21, matrix products: 14.5 us -> 20.8 us  [rows_dot(): lax.dot_general(left, right, (((left_dim,), (right_dim,)), ((), ())), pre...]
    transpose x3 -> x0, local copies, waits for them, and re-layouts: 5.13 us -> none  [gather_rows(): return jnp.swapaxes(blocks, 0, 1).reshape(-1, rows.shape[1])]
    unnamed x96 -> x95, local copies, waits for them, and re-layouts: 21.3 us -> 18.5 us
    reduce_sum x10 -> x13, other arithmetic: 12.5 us -> 12.5 us  [add_up(): return jnp.sum(blocks.astype(jnp.float32), axis=0)]
  transfers between devices with their start and end apart: 13 -> 9, of which waited for: 3 -> 0; matrix products, arithmetic and copies ran while one was open for 17% -> 12% of each run, Pallas kernels for 42% -> 11%
where the time goes in v3:
time: 282 us; the launch traced here: 280 us
  Pallas kernels  177 us (63%)
  other arithmetic  41.4 us (15%)
  local copies, waits for them, and re-layouts  28.3 us (10%)
  matrix products  20.8 us (7%)
  starting transfers between devices  10.6 us (4%)
    pallas_call x9, Pallas kernels, exchange(): pl.pallas_call(lambda *refs: exchange_kernel(kinds, greet, counts, *refs)...  136 us
    pallas_call x1, Pallas kernels, staged_gather(): pl.pallas_call(lambda *refs: staged_kernel(plans, greeted, *refs), out_sh...  31.6 us
    dot_general x21, matrix products, rows_dot(): lax.dot_general(left, right, (((left_dim,), (right_dim,)), ((), ())), pre...  20.8 us
    unnamed x95, local copies, waits for them, and re-layouts  18.5 us
    reduce_sum x13, other arithmetic, add_up(): return jnp.sum(blocks.astype(jnp.float32), axis=0)  12.5 us
    ppermute x7, starting transfers between devices, shifted(): lax.ppermute(array, axis, [(here, (here + offset) % count) for here in ra...  9.28 us
  transfers between devices with their start and end apart: 9, of which 0 were waited for; matrix products, arithmetic and copies ran while one was open for 12% of the time, Pallas kernels for 11%

profile of v3, /device:TPU:0, one launch (start us, length us, event | category | flops | bytes accessed | tf_op | source)
XLA Modules:
  0.0 280.1 jit_solution(2741251375942671989)
XLA Ops:
  0.6 0.8 pad_maximum_fusion.8
  2.1 0.9 slice_reduce_fusion
  4.5 1.3 pad_maximum_fusion.9.refs_1_
  5.8 1.7 pad_maximum_fusion.7
  8.1 31.6 %first_gather.1 = (bf16[2,2,2,128,640]{4,3,2,1,0:T(8,128)(2,1)}, bf16[2,2,2,4,16,640]{5,4,3,2,1,0:T(8,128)(2,1)}, bf16[2,4,64,640]{3,2,1,0:T(8,128)(2,1)}, s32[2,4,128]{2,1,0:T(4,128)}) custom-call(bf16[128,640]{1,0:T(8,128)(2,1)} %refs_0_.1, bf16[16,640]{1,0:T(8,128)(2,1)} %pad_maximum_fusion.9.refs_1_, bf16[64,640]{1,0:T(8,128)(2,1)} %copy-done.40, ...), custom_call_target="tpu_custom_call" | custom-call | tf_op jit(solution)/shard_map/first_gather/pallas_call | solution.py:284
  39.7 1.7 multiply_reduce_fusion
  44.4 0.9 collective-permute-start.2
  45.3 2.9 %collective-permute-start.3 = (bf16[192,640]{1,0:T(8,128)(2,1)}, bf16[192,640]{1,0:T(8,128)(2,1)}, u32[]{:S(2)}, u32[]{:S(2)}) collective-permute-start(bf16[192,640]{1,0:T(8,128)(2,1)} %pad_maximum_fusion.7), channel_id=1, source_target_pairs={{0,24},{8,0},{16,8},{24,16},{1,25},{9,1},{17,9},{25,17},{2,26},{10... | collective-permute-start | bytes 737288 | tf_op jit(solution)/shard_map/ppermute | solution.py:302
  48.2 2.4 collective-permute-start.4
  52.4 2.1 multiply_cosine_fusion
  56.4 1.4 fusion.63
  57.8 1.3 convolution_convert_fusion
  59.1 9.9 %branch_scatter.1 = bf16[4,128,640]{2,1,0:T(8,128)(2,1)} custom-call(bf16[4,128,640]{2,1,0:T(8,128)(2,1)} %bitcast.120), custom_call_target="tpu_custom_call" | custom-call | tf_op jit(solution)/shard_map/branch_scatter/pallas_call | solution.py:161
  69.0 1.2 convert_reduce_fusion.4
  70.9 1.1 multiply_reduce_fusion.13
  73.6 1.7 slice_dynamic-update-slice_fusion.13
  75.2 1.0 collective-permute-start.5
  76.3 1.0 collective-permute-start.6
  77.3 1.0 collective-permute-start.7
  78.3 1.7 slice_dynamic-update-slice_fusion.12
  80.0 1.7 slice_dynamic-update-slice_fusion.11
  81.6 1.7 slice_dynamic-update-slice_fusion.10
  83.3 1.7 slice_dynamic-update-slice_fusion.9
  85.0 10.5 %mlp_gather.1 = bf16[4,128,640]{2,1,0:T(8,128)(2,1)} custom-call(bf16[128,640]{1,0:T(8,128)(2,1)} %multiply_multiply_fusion.2.refs_0_), custom_call_target="tpu_custom_call" | custom-call | tf_op jit(solution)/shard_map/mlp_gather/pallas_call | solution.py:161
  95.5 1.7 slice_dynamic-update-slice_fusion.2
  97.1 1.7 slice_dynamic-update-slice_fusion.1
  98.8 1.7 slice_dynamic-update-slice_fusion
  100.5 4.2 %mlp_forward.1 = (f32[512,512]{1,0:T(8,128)}, f32[512,512]{1,0:T(8,128)}, bf16[512,512]{1,0:T(8,128)(2,1)}, bf16[512,640]{1,0:T(8,128)(2,1)}) custom-call(bf16[512,640]{1,0:T(8,128)(2,1)} %bitcast.112, bf16[512,640]{1,0:T(8,128)(2,1)} %get-tuple-element.109.gate_ref, bf16[512,640]{1,0:T(8,128)(2,1)} %get-tuple-element.108.up_ref, ...), custom_call_target="tpu_custom_call" | custom-call | tf_op jit(solution)/shard_map/mlp_forward/pallas_call | solution.py:468
  104.7 11.5 %down_scatter.1 = bf16[4,128,640]{2,1,0:T(8,128)(2,1)} custom-call(bf16[4,128,640]{2,1,0:T(8,128)(2,1)} %bitcast.132), custom_call_target="tpu_custom_call" | custom-call | tf_op jit(solution)/shard_map/down_scatter/pallas_call | solution.py:161
  116.1 1.2 convert_reduce_fusion.3
  117.5 1.1 fusion.30
  118.6 2.0 fusion.27
  120.5 11.3 %grad_down_gather.1 = bf16[4,128,640]{2,1,0:T(8,128)(2,1)} custom-call(bf16[128,640]{1,0:T(8,128)(2,1)} %get-tuple-element.105.refs_0_), custom_call_target="tpu_custom_call" | custom-call | tf_op jit(solution)/shard_map/grad_down_gather/pallas_call | solution.py:161
  131.8 2.7 convolution_convert_fusion.1
  134.5 5.2 %mlp_backward.1 = (bf16[512,512]{1,0:T(8,128)(2,1)}, bf16[512,512]{1,0:T(8,128)(2,1)}, bf16[512,640]{1,0:T(8,128)(2,1)}) custom-call(bf16[512,640]{1,0:T(8,128)(2,1)} %bitcast.116, bf16[512,640]{1,0:T(8,128)(2,1)} %get-tuple-element.109.gate_ref, bf16[512,640]{1,0:T(8,128)(2,1)} %get-tuple-element.108.up_ref, bf16[512,640]{1,0:T(8,128)(2,1)} %get-tuple-element.107.down_ref, ...), custom_call_target="tpu_custom_call" | custom-call | tf_op jit(solution)/shard_map/mlp_backward/pallas_call | solution.py:484
  139.8 1.9 convolution_convert_fusion.2
  141.7 1.8 convolution_convert_fusion.3
  143.7 1.5 fusion.58
  145.2 17.7 %grad_mlp_scatter.1 = (bf16[4,128,640]{2,1,0:T(8,128)(2,1)}, bf16[2,2,192,640]{3,2,1,0:T(8,128)(2,1)}) custom-call(bf16[4,128,640]{2,1,0:T(8,128)(2,1)} %bitcast.129, bf16[2,2,192,640]{3,2,1,0:T(8,128)(2,1)} %get-tuple-element.91.refs_1_), custom_call_target="tpu_custom_call" | custom-call | tf_op jit(solution)/shard_map/grad_mlp_scatter/pallas_call | solution.py:161
  162.9 1.2 convert_reduce_fusion.2
  164.1 1.1 multiply_reduce_fusion.8
  165.2 1.3 multiply_reduce_fusion.9
  166.6 0.8 subtract_convert_fusion.2.refs_0_
  167.4 16.1 %grad_branch_gather.1 = (bf16[4,128,640]{2,1,0:T(8,128)(2,1)}, bf16[2,2,192,640]{3,2,1,0:T(8,128)(2,1)}) custom-call(bf16[128,640]{1,0:T(8,128)(2,1)} %subtract_convert_fusion.2.refs_0_, bf16[2,2,192,640]{3,2,1,0:T(8,128)(2,1)} %get-tuple-element.90.refs_1_), custom_call_target="tpu_custom_call" | custom-call | tf_op jit(solution)/shard_map/grad_branch_gather/pallas_call | solution.py:161
  183.5 1.8 multiply_reduce_fusion.6
  188.4 2.1 fusion.15
  193.3 1.3 copy-done.2
  196.5 1.2 convert_element_type.185
  198.3 1.3 convolution_convert_fusion.6
  199.6 1.3 convolution_convert_fusion.7
  200.9 1.6 reduce.5
  203.2 1.0 maximum_bitcast_fusion.refs_1_
  204.2 2.0 maximum_bitcast_fusion.1.refs_2_
  206.1 1.1 pad_maximum_fusion.2.refs_3_
  207.2 34.5 %last_scatter.1 = (bf16[8,128,640]{2,1,0:T(8,128)(2,1)}, bf16[2,4,64,640]{3,2,1,0:T(8,128)(2,1)}, bf16[8,4,16,640]{3,2,1,0:T(8,128)(2,1)}, bf16[4,192,640]{2,1,0:T(8,128)(2,1)}) custom-call(bf16[8,128,640]{2,1,0:T(8,128)(2,1)} %bitcast.103, bf16[2,4,64,640]{3,2,1,0:T(8,128)(2,1)} %maximum_bitcast_fusion.refs_1_, ...), custom_call_target="tpu_custom_call" | custom-call | tf_op jit(solution)/shard_map/last_scatter/pallas_call | solution.py:161
  241.7 1.7 convert_reduce_fusion
  243.7 0.9 reduce_sum.342.refs_1_
  246.0 15.3 %depth_exchange.1 = (f32[4,8,640]{2,1,0:T(8,128)}, bf16[4,64,640]{2,1,0:T(8,128)(2,1)}, bf16[4,16,640]{2,1,0:T(8,128)(2,1)}) custom-call(f32[8,640]{1,0:T(8,128)} %concatenate.67.refs_0_, bf16[4,64,640]{2,1,0:T(8,128)(2,1)} %reduce_sum.342.refs_1_, bf16[4,16,640]{2,1,0:T(8,128)(2,1)} %reduce_sum.343.refs_2_), custom_call_target="tpu_custom_call" | custom-call | tf_op jit(solution)/shard_map/depth_exchange/pallas_call | solution.py:161
  261.2 1.1 reduce_sum.346
  263.0 0.9 convert_reduce_fusion.5
  264.0 0.8 fusion.60
  264.8 0.8 fusion.35
  266.9 9.8 %gain_gather.1 = f32[8,8,640]{2,1,0:T(8,128)} custom-call(f32[8,640]{1,0:T(8,128)} %reduce_sum.344.refs_0_), custom_call_target="tpu_custom_call" | custom-call | tf_op jit(solution)/shard_map/gain_gather/pallas_call | solution.py:161
  276.7 0.9 reduce_sum.345
  (171 shorter events, 26.6 us)
Async XLA Ops:
  1.5 6.0 %collective-permute-start = (bf16[64,640]{1,0:T(8,128)(2,1)S(1)}, bf16[64,640]{1,0:T(8,128)(2,1)S(1)}, u32[]{:S(2)}, u32[]{:S(2)}) collective-permute-start(bf16[64,640]{1,0:T(8,128)(2,1)S(1)} %pad_maximum_fusion.8), channel_id=1, source_target_pairs={{0,0},{1,4},{2,8},{3,12},{4,16},{5,20},{6,24},{7,28},{8,1},{9,5},{... | collective-permute-start | bytes 245768 | tf_op jit(solution)/shard_map/ppermute | solution.py:387
  7.5 0.6 copy-start.40
  39.7 1.8 copy-start
  41.5 1.1 copy-start.34
  42.0 2.1 copy-start.23
  42.6 0.9 copy-start.11
  43.5 12.9 %copy-start.17 = (bf16[1024,256]{1,0:T(8,128)(2,1)}, bf16[1024,256]{1,0:T(8,128)(2,1)S(1)}, u32[]{:S(2)}) copy-start(bf16[1024,256]{1,0:T(8,128)(2,1)S(1)} %convolution_convert_fusion.5) | copy-start | bytes 1572868
  44.1 6.5 %copy-start.42 = (s32[2,4,128]{2,1,0:T(4,128)S(1)}, s32[2,4,128]{2,1,0:T(4,128)}, u32[]{:S(2)}) copy-start(s32[2,4,128]{2,1,0:T(4,128)} %get-tuple-element.44) | copy-start | bytes 12292
  44.1 6.5 %copy-start.31 = (bf16[2,4,64,640]{3,2,1,0:T(8,128)(2,1)S(1)}, bf16[2,4,64,640]{3,2,1,0:T(8,128)(2,1)}, u32[]{:S(2)}) copy-start(bf16[2,4,64,640]{3,2,1,0:T(8,128)(2,1)} %get-tuple-element.43) | copy-start | bytes 1966084
  44.4 29.2 %collective-permute-start.1 = (bf16[192,640]{1,0:T(8,128)(2,1)}, bf16[192,640]{1,0:T(8,128)(2,1)}, u32[]{:S(2)}, u32[]{:S(2)}) collective-permute-start(bf16[192,640]{1,0:T(8,128)(2,1)} %pad_maximum_fusion.7), channel_id=1, source_target_pairs={{0,8},{8,16},{16,24},{24,0},{1,9},{9,17},{17,25},{25,1},{2,10},{10... | collective-permute-start | bytes 737288 | tf_op jit(solution)/shard_map/ppermute | solution.py:302
  44.4 29.1 %collective-permute-start.2 = (bf16[192,640]{1,0:T(8,128)(2,1)}, bf16[192,640]{1,0:T(8,128)(2,1)}, u32[]{:S(2)}, u32[]{:S(2)}) collective-permute-start(bf16[192,640]{1,0:T(8,128)(2,1)} %pad_maximum_fusion.7), channel_id=1, source_target_pairs={{0,16},{8,24},{16,0},{24,8},{1,17},{9,25},{17,1},{25,9},{2,18},{10... | collective-permute-start | bytes 737288 | tf_op jit(solution)/shard_map/ppermute | solution.py:302
  45.3 28.3 %collective-permute-start.3 = (bf16[192,640]{1,0:T(8,128)(2,1)}, bf16[192,640]{1,0:T(8,128)(2,1)}, u32[]{:S(2)}, u32[]{:S(2)}) collective-permute-start(bf16[192,640]{1,0:T(8,128)(2,1)} %pad_maximum_fusion.7), channel_id=1, source_target_pairs={{0,24},{8,0},{16,8},{24,16},{1,25},{9,1},{17,9},{25,17},{2,26},{10... | collective-permute-start | bytes 737288 | tf_op jit(solution)/shard_map/ppermute | solution.py:302
  48.2 25.3 %collective-permute-start.4 = (bf16[192,640]{1,0:T(8,128)(2,1)}, bf16[192,640]{1,0:T(8,128)(2,1)}, u32[]{:S(2)}, u32[]{:S(2)}) collective-permute-start(bf16[192,640]{1,0:T(8,128)(2,1)} %pad_maximum_fusion.7), channel_id=1, source_target_pairs={{0,4},{4,0},{1,5},{5,1},{2,6},{6,2},{3,7},{7,3},{8,12},{12,8},{9,1... | collective-permute-start | bytes 737288 | tf_op jit(solution)/shard_map/ppermute | solution.py:302
  50.7 0.7 copy-start.6
  50.8 7.1 %copy-start.8 = (bf16[8,32,640]{2,1,0:T(8,128)(2,1)}, bf16[8,32,640]{2,1,0:T(8,128)(2,1)S(1)}, u32[]{:S(2)}) copy-start(bf16[8,32,640]{2,1,0:T(8,128)(2,1)S(1)} %get-tuple-element.100) | copy-start | bytes 983044
  51.0 1.5 copy-start.1
  52.0 2.6 copy-start.3
  54.6 1.1 copy-start.19
  54.6 1.1 copy-start.21
  54.6 1.1 copy-start.36
  54.6 1.1 copy-start.38
  54.8 1.0 copy-start.25
  54.8 1.1 copy-start.27
  57.8 1.3 copy-start.15
  72.0 0.7 copy-start.5
  75.2 20.2 %collective-permute-start.5 = (bf16[192,640]{1,0:T(8,128)(2,1)}, bf16[192,640]{1,0:T(8,128)(2,1)}, u32[]{:S(2)}, u32[]{:S(2)}) collective-permute-start(bf16[192,640]{1,0:T(8,128)(2,1)} %collective-permute-done.1), channel_id=1, source_target_pairs={{0,4},{4,0},{1,5},{5,1},{2,6},{6,2},{3,7},{7,3},{8,12},{12,8},{9,1... | collective-permute-start | bytes 737288 | tf_op jit(solution)/shard_map/ppermute | solution.py:302
  76.3 20.9 %collective-permute-start.6 = (bf16[192,640]{1,0:T(8,128)(2,1)}, bf16[192,640]{1,0:T(8,128)(2,1)}, u32[]{:S(2)}, u32[]{:S(2)}) collective-permute-start(bf16[192,640]{1,0:T(8,128)(2,1)} %collective-permute-done.2), channel_id=1, source_target_pairs={{0,4},{4,0},{1,5},{5,1},{2,6},{6,2},{3,7},{7,3},{8,12},{12,8},{9,1... | collective-permute-start | bytes 737288 | tf_op jit(solution)/shard_map/ppermute | solution.py:302
  77.3 21.5 %collective-permute-start.7 = (bf16[192,640]{1,0:T(8,128)(2,1)}, bf16[192,640]{1,0:T(8,128)(2,1)}, u32[]{:S(2)}, u32[]{:S(2)}) collective-permute-start(bf16[192,640]{1,0:T(8,128)(2,1)} %collective-permute-done.3), channel_id=1, source_target_pairs={{0,4},{4,0},{1,5},{5,1},{2,6},{6,2},{3,7},{7,3},{8,12},{12,8},{9,1... | collective-permute-start | bytes 737288 | tf_op jit(solution)/shard_map/ppermute | solution.py:302
  139.8 3.8 %copy-start.35 = (bf16[512,640]{1,0:T(8,128)(2,1)S(1)}, bf16[512,640]{1,0:T(8,128)(2,1)}, u32[]{:S(2)}) copy-start(bf16[512,640]{1,0:T(8,128)(2,1)} %convolution_convert_fusion.1) | copy-start | bytes 1966084
  162.9 3.7 %copy-start.43 = (f32[128]{0:T(128)S(1)}, f32[128]{0:T(128)}, u32[]{:S(2)}) copy-start(f32[128]{0:T(128)} %get-tuple-element.146) | copy-start | bytes 1540
  166.5 0.8 copy-start.9
  183.5 2.4 copy-start.18
  185.9 1.0 copy-start.26
  185.9 1.0 copy-start.28
  186.9 0.9 copy-start.37
  186.9 1.0 copy-start.39
  190.5 1.1 copy-start.12
  191.6 1.0 copy-start.20
  191.6 1.2 copy-start.22
  191.6 1.4 copy-start.4
  192.8 1.8 copy-start.2
  195.1 1.0 copy-start.7
  196.5 1.8 copy-start.24
  199.6 2.9 %copy-start.29 = (bf16[2,2,192,640]{3,2,1,0:T(8,128)(2,1)S(1)}, bf16[2,2,192,640]{3,2,1,0:T(8,128)(2,1)}, u32[]{:S(2)}) copy-start(bf16[2,2,192,640]{3,2,1,0:T(8,128)(2,1)} %get-tuple-element.62) | copy-start | bytes 2949124
  200.9 1.9 copy-start.13
  200.9 1.9 copy-start.16
  207.2 36.2 %copy-start.14 = (bf16[128,640]{1,0:T(8,128)(2,1)S(1)}, bf16[128,640]{1,0:T(8,128)(2,1)}, u32[]{:S(2)}) copy-start(bf16[128,640]{1,0:T(8,128)(2,1)} %refs_0_.1) | copy-start | bytes 491524
  241.7 2.0 copy-start.33
  241.7 2.9 %copy-start.32 = (bf16[8,4,16,640]{3,2,1,0:T(8,128)(2,1)S(1)}, bf16[8,4,16,640]{3,2,1,0:T(8,128)(2,1)}, u32[]{:S(2)}) copy-start(bf16[8,4,16,640]{3,2,1,0:T(8,128)(2,1)} %get-tuple-element.66) | copy-start | bytes 1966084
  241.7 22.1 %copy-start.30 = (bf16[4,192,640]{2,1,0:T(8,128)(2,1)S(1)}, bf16[4,192,640]{2,1,0:T(8,128)(2,1)}, u32[]{:S(2)}) copy-start(bf16[4,192,640]{2,1,0:T(8,128)(2,1)} %get-tuple-element.70) | copy-start | bytes 2949124
  244.6 20.2 %copy-start.10 = (f32[128,640]{1,0:T(8,128)S(1)}, f32[128,640]{1,0:T(8,128)}, u32[]{:S(2)}) copy-start(f32[128,640]{1,0:T(8,128)} %copy-done.9) | copy-start | bytes 983044
  261.2 5.0 %copy-start.41 = (f32[4,8,640]{2,1,0:T(8,128)S(1)}, f32[4,8,640]{2,1,0:T(8,128)}, u32[]{:S(2)}) copy-start(f32[4,8,640]{2,1,0:T(8,128)} %get-tuple-element.67) | copy-start | bytes 245764
  262.3 16.5 %collective-permute-start.8 = (bf16[64,640]{1,0:T(8,128)(2,1)S(1)}, bf16[64,640]{1,0:T(8,128)(2,1)S(1)}, u32[]{:S(2)}, u32[]{:S(2)}) collective-permute-start(bf16[64,640]{1,0:T(8,128)(2,1)S(1)} %reduce_sum.346), channel_id=1, source_target_pairs={{0,0},{4,1},{8,2},{12,3},{16,4},{20,5},{24,6},{28,7},{1,8},{5,9},{... | collective-permute-start | bytes 245768 | tf_op jit(solution)/shard_map/ppermute | solution.py:606
